TPU v7x, 32 devices: a whole 2x2x4 slice. The times are simulated.
32 devices in a mesh: dp: 4 (over z), seq: 8 (over y, x, core).
Axes of the slice: x: 2, y: 2, z: 4, core: 2. Of those that a mesh axis runs over, the one named last changes fastest.
Arguments:
- inputs: bfloat16 [4, 2048, 768], P('dp', 'seq'), may hold values from -6 to 6
- cotangent: float32 [4, 2048, 768], P('dp', 'seq'), may hold values from -6 to 6
- doc_lengths: int32 [4, 8], P('dp'), may hold values from 1 to 1920, 2048 in all within a row
- doc_labels: int32 [4, 8], P('dp'), may hold values from 0 to 2
- query_weight: bfloat16 [768, 768], P('seq'), may hold values from -0.3125 to 0.3125
- query_bias: bfloat16 [768], P('seq'), may hold values from -4 to 4
- key_weight: bfloat16 [768, 768], P('seq'), may hold values from -0.3125 to 0.3125
- value_weight: bfloat16 [768, 768], P('seq'), may hold values from -0.21875 to 0.21875
- value_bias: bfloat16 [768], P('seq'), may hold values from -0.75 to 0.75
- proj_weight: bfloat16 [768, 768], P('seq'), may hold values from -0.625 to 0.625
- proj_bias: bfloat16 [768], P('seq'), may hold values from -4 to 4
- norm_gain: bfloat16 [768], P('seq'), may hold values from 0.099609375 to 1.8984375
- norm_shift: bfloat16 [768], P('seq'), may hold values from -4 to 4
- up_weight: bfloat16 [768, 3072], P('seq'), may hold values from -0.21875 to 0.21875
- up_bias: bfloat16 [3072], P('seq'), may hold values from -4 to 4
- down_weight: bfloat16 [3072, 768], P('seq'), may hold values from -0.109375 to 0.109375
- down_bias: bfloat16 [768], P('seq'), may hold values from -4 to 4
- final_gain: bfloat16 [768], P('seq'), may hold values from 0.099609375 to 1.8984375
- final_shift: bfloat16 [768], P('seq'), may hold values from -4 to 4
- pool_weight: bfloat16 [768, 768], P('seq'), may hold values from -0.21875 to 0.21875
- pool_bias: bfloat16 [768], P('seq'), may hold values from -4 to 4
- class_weight: bfloat16 [768, 3], P('seq'), may hold values from -0.4375 to 0.4375
- class_bias: bfloat16 [3], replicated, may hold values from -6 to 6
Outputs:
- output: bfloat16 [4, 2048, 768], P('dp', 'seq')
- logits: float32 [4, 8, 3], P('dp')
- input_grad: float32 [4, 2048, 768], P('dp', 'seq')
- query_wgrad: float32 [768, 768], P('seq')
- query_bgrad: float32 [768], P('seq')
- key_wgrad: float32 [768, 768], P('seq')
- value_wgrad: float32 [768, 768], P('seq')
- value_bgrad: float32 [768], P('seq')
- proj_wgrad: float32 [768, 768], P('seq')
- proj_bgrad: float32 [768], P('seq')
- norm_ggrad: float32 [768], P('seq')
- norm_sgrad: float32 [768], P('seq')
- up_wgrad: float32 [768, 3072], P('seq')
- up_bgrad: float32 [3072], P('seq')
- down_wgrad: float32 [3072, 768], P('seq')
- down_bgrad: float32 [768], P('seq')
- final_ggrad: float32 [768], P('seq')
- final_sgrad: float32 [768], P('seq')
- pool_wgrad: float32 [768, 768], P('seq')
- pool_bgrad: float32 [768], P('seq')
- class_wgrad: float32 [768, 3], P('seq')
- class_bgrad: float32 [3], replicated
Inputs may be any that keep to these rules, and one draw needn't show every extreme that they name: `doc_lengths`: in each sequence the 8 lengths sum to 2048, and one document has exactly 1920 tokens.
All inputs are finite; a program needn't handle non-finite values.
Results may differ from a plain program's by a relative error of at most 0.025.
Values may be sent and summed in bfloat16 or wider, within the bound.
No kernel may reach another device: no remote copies, remote signals or barrier semaphores. Data moves between devices by JAX's collectives and lax.ppermute only.
A program may use at most 192 MiB of HBM per device.

v0:
```python
import functools

import jax
import jax.numpy as jnp
from jax import lax
from jax.experimental import pallas as pl
from jax.experimental.pallas import tpu as pltpu
from jax.sharding import PartitionSpec as P

D = 768
HEADS = 12
HEAD_DIM = 64
FF = 3072
CLASSES = 3
PAIR = 2 * HEAD_DIM
ROWS = 256
EPSILON = 1e-06
FAR = -1e30
LIMIT = 56 * 1024 * 1024
F32, BF16 = jnp.float32, jnp.bfloat16

QUERY_B, VALUE_B, PROJ_B, NORM_G, NORM_S, DOWN_B, FINAL_G, FINAL_S, POOL_B, CLASS_W, UP_B = (
    0, 1, 2, 3, 4, 5, 6, 7, 8, 9, 12,
)
TABLE = 16


def swap(value, partner):
    dp, seq = lax.axis_size("dp"), lax.axis_size("seq")
    pairs = []
    for z in range(dp):
        for i in range(seq):
            to_z, to_i = partner(z, i)
            pairs.append((z * seq + i, to_z * seq + to_i))
    return lax.ppermute(value, ("dp", "seq"), pairs)


def along(bit):
    return lambda z, i: (z, i ^ bit)


def is_small():
    return lax.axis_size("seq") == 8 and lax.axis_size("dp") == 4


class Shared:
    def __init__(self, shard, role):
        self.shard, self.role = shard, role

    def near(self):
        role = self.role
        self.one = swap(self.shard, lambda z, i: (z, i ^ (2 if (z + role) % 2 == 0 else 4)))

    def far(self):
        role = self.role
        self.both = swap(self.one, lambda z, i: (z, i ^ (4 if (z + role) % 2 == 0 else 2)))

    def cross(self):
        self.crossed = [swap(block, along(1)) for block in (self.shard, self.one)]

    def cross_both(self):
        self.middle = swap(self.both, along(1))

    def rest(self):
        self.other = swap(self.one, lambda z, i: (z ^ 1, i))

    def rest_direct(self):
        role = self.role
        self.other = swap(self.shard, lambda z, i: (z, i ^ (4 if (z + role) % 2 == 0 else 2)))

    def finish(self):
        last = swap(self.other, along(1))
        return [self.shard, self.one, self.both, self.other, *self.crossed, self.middle, last]

    def owners(self):
        me, z = lax.axis_index("seq"), lax.axis_index("dp")
        near = jnp.where((z + self.role) % 2 == 0, 2, 4)
        owners = [me, me ^ near, me ^ 6, me ^ (6 - near)]
        owners = [owners[k] for k in (0, 1, 2, 3)] + [owners[k] ^ 1 for k in (0, 1, 2, 3)]
        return jnp.stack(owners)


def gather_tokens(tokens):
    if not is_small():
        return [tokens]
    far = swap(tokens, along(6))
    return [tokens, swap(tokens, along(2)), swap(tokens, along(4)), far]


def exchange(pieces):
    return [pieces[0]] + [swap(pieces[s], along(2 * s)) for s in range(1, len(pieces))]


def slot_owners():
    if not is_small():
        return jnp.arange(lax.axis_size("seq"), dtype=jnp.int32)
    return lax.axis_index("seq") ^ jnp.array([0, 2, 4, 6, 1, 3, 5, 7], jnp.int32)


def add(*terms):
    return functools.reduce(jnp.add, [term.astype(F32) for term in terms])


class Scatter:
    def __init__(self, parts):
        self.firsts, self.seconds, self.own = parts[0:2], parts[2:4], parts[4]
        self.comes = [swap(a, along(bit)) for a, bit in zip(self.firsts, (2, 4))]

    def combine(self, *earlier):
        seconds = after(self.seconds, *earlier)
        self.sends = [add(a, come[1]).astype(BF16) for a, come in zip(seconds, self.comes)]

    def turn(self):
        self.lasts = [swap(a, along(bit)) for a, bit in zip(self.sends, (4, 2))]

    def total(self):
        half = self.own.shape[0] // 2
        owns = (self.own[:half], self.own[half:])
        return jnp.concatenate(
            [add(own, come[0], last) for own, come, last in zip(owns, self.comes, self.lasts)]
        )


def after(values, *others):
    return lax.optimization_barrier((values, others))[0]


class SumDp:
    def __init__(self, shard):
        z = lax.axis_index("dp")
        half = shard.shape[0] // 2
        self.low = jnp.logical_or(z == 0, z == 3)
        first, second = shard[:half], shard[half:]
        self.keep = jnp.where(self.low, first, second)
        self.come = swap(
            jnp.where(self.low, second, first).astype(BF16), lambda z, i: (z ^ 1, i)
        )

    def across(self):
        self.pair = add(self.keep, self.come).astype(BF16)
        self.cross = swap(self.pair, lambda z, i: (z ^ 3, i))

    def finish(self):
        self.whole = add(self.pair, self.cross).astype(BF16)
        self.last = swap(self.whole, lambda z, i: (z ^ 1, i))

    def back(self):
        total, come = self.whole, self.last
        low = self.low
        return jnp.concatenate(
            [jnp.where(low, total, come), jnp.where(low, come, total)], axis=0
        ).astype(F32)


def sum_dp(shard):
    if not is_small():
        return lax.psum(shard.astype(BF16), "dp").astype(F32)
    total = SumDp(shard)
    total.across()
    total.finish()
    return total.back()


def sum_seq(value):
    if not is_small():
        return lax.psum(value, "seq")
    for bit in (1, 2, 4):
        value = value + swap(value, along(bit))
    return value


def sum_all(value):
    value = sum_seq(value)
    if not is_small():
        return lax.psum(value, "dp")
    for bit in (1, 2):
        value = value + swap(value, lambda z, i: (z ^ bit, i))
    return value


def stack_dp(value):
    if not is_small():
        return lax.all_gather(value, "dp", axis=0, tiled=True)
    for bit in (1, 2):
        value = jnp.concatenate([value, swap(value, lambda z, i: (z ^ bit, i))], axis=0)
    return value


def dot(left, right, contract=((1,), (0,))):
    return lax.dot_general(left, right, (contract, ((), ())), preferred_element_type=F32)


def call(body, name, micros, **kwargs):
    return pl.pallas_call(
        body,
        name=name,
        cost_estimate=pl.CostEstimate(
            flops=int(micros * 1.1e9), transcendentals=0, bytes_accessed=int(micros * 1e6)
        ),
        compiler_params=pltpu.CompilerParams(vmem_limit_bytes=LIMIT),
        **kwargs,
    )


VMEM = pl.BlockSpec(memory_space=pltpu.VMEM)
ANY = pl.BlockSpec(memory_space=pl.ANY)
SMEM = pl.BlockSpec(memory_space=pltpu.SMEM)


def start(copies):
    for copy in copies:
        copy.start()
    return copies


def wait(copies):
    for copy in copies:
        copy.wait()


def like(arrays):
    return [pltpu.VMEM(a.shape, a.dtype) for a in arrays]


def block_copies(places, line, refs, target, sems, part=None):
    copies = []
    for slot, ref in enumerate(refs):
        source = ref if part is None else ref.at[part]
        rows = source.shape[-2]
        first = pl.multiple_of(places[line, slot] * rows, rows)
        if len(source.shape) == 3:
            place = target.at[:, pl.ds(first, rows), :]
        else:
            place = target.at[pl.ds(first, rows), :]
        copies.append(pltpu.make_async_copy(source, place, sems.at[slot]))
    return start(copies)


def weight_refs(weights):
    return [ref.at[s] for ref in weights for s in range(ref.shape[0])]


def qkv_kernel(blocks, sides, places, *refs):
    tokens, refs = refs[:blocks], refs[blocks:]
    weights, (bias, query, keyval, held, sems) = refs[:sides], refs[sides:]
    wait(block_copies(places, 0, weight_refs(weights), held, sems))
    for s in range(query.shape[0]):
        rows = tokens[s][...]
        keyval[0, s] = dot(rows, held[1]).astype(BF16)
        keyval[1, s] = (dot(rows, held[2]) + bias[1:2]).astype(BF16)
        query[s] = (dot(rows, held[0]) + bias[0:1]).astype(BF16)


def qkv_project(places, tokens, weights, bias):
    slots = len(tokens)
    lanes = weights[0].shape[-1]
    out = jax.ShapeDtypeStruct((slots, ROWS, lanes), BF16)
    pair = jax.ShapeDtypeStruct((2, slots, ROWS, lanes), BF16)
    return call(
        functools.partial(qkv_kernel, len(tokens), len(weights)),
        "qkv",
        5,
        out_shape=(out, pair),
        in_specs=[SMEM] + [VMEM] * len(tokens) + [ANY] * len(weights) + [VMEM],
        out_specs=(VMEM,) * 2,
        scratch_shapes=[
            pltpu.VMEM((3, D, lanes), BF16),
            pltpu.SemaphoreType.DMA((len(weights) * weights[0].shape[0],)),
        ],
    )(places, *tokens, *weights, bias)


def turn_kernel(*refs):
    for s, ref in enumerate(refs[:-1]):
        turn_wide(ref, refs[-1].at[:, s * ROWS : (s + 1) * ROWS])


def turn_tokens(tokens):
    return call(
        turn_kernel,
        "turn_tokens",
        2,
        out_shape=jax.ShapeDtypeStruct((D, len(tokens) * ROWS), BF16),
        in_specs=[VMEM] * len(tokens),
        out_specs=VMEM,
    )(*tokens)


def left_half(shape):
    return lax.broadcasted_iota(jnp.int32, shape, len(shape) - 1) < HEAD_DIM


def split3(value):
    high = value.astype(BF16).astype(F32)
    middle = (value - high).astype(BF16).astype(F32)
    low = (value - high - middle).astype(BF16).astype(F32)
    return high, middle, low


def spread3(value, docs, shape):
    lane = lax.broadcasted_iota(jnp.int32, shape, 1) % HEAD_DIM
    high, middle, low = split3(value)
    return jnp.where(
        lane == docs, high, jnp.where(lane == docs + 1, middle, jnp.where(lane == docs + 2, low, 0.0))
    )


STEP = 512


def eye(size):
    shape = (size, size)
    same = lax.broadcasted_iota(jnp.int32, shape, 0) == lax.broadcasted_iota(jnp.int32, shape, 1)
    return jnp.where(same, 1.0, 0.0).astype(BF16)


def turn(value):
    return dot(eye(value.shape[1]), value, ((1,), (1,))).astype(BF16)


def turn_wide(value, target, first=0):
    for at in range(0, value.shape[1], PAIR * 2):
        block = value[:, at : at + PAIR * 2]
        target[first + at : first + at + block.shape[1]] = turn(block)


def fill_keys(keyvals, feature_k, keys, values, mine):
    at = 0
    for ref in keyvals:
        for index in range(ref.shape[1]):
            rows = slice(at, at + ROWS)
            keys[rows] = jnp.where(mine, ref[0, index], feature_k[at // ROWS])
            values[rows] = jnp.where(mine, ref[1, index], feature_k[at // ROWS])
            at += ROWS


def for_heads(odd, body):
    if not odd:
        body(2)
        return
    tile = pl.program_id(0)
    pl.when(tile < pl.num_programs(0) - 1)(lambda: body(2))
    pl.when(tile == pl.num_programs(0) - 1)(lambda: body(1))


def attend_kernel(sides, docs, odd, *refs):
    query, feature_q, feature_k = refs[:3]
    keyvals = refs[3 : 3 + sides]
    slots, length = feature_q.shape[0], feature_k.shape[0] * ROWS
    rest = refs[3 + sides :]
    wide, total, lows, (keys, values, scores) = rest[0], rest[1], rest[2:-3], rest[-3:]
    left = left_half((ROWS, PAIR))
    sides_of = (left, jnp.logical_not(left))

    def body(heads):
        for head in range(heads):
            fill_keys(keyvals, feature_k, keys.at[head], values.at[head], sides_of[head])
        units = [(slot, head) for slot in range(slots) for head in range(heads)]

        def queries(unit):
            slot, head = unit
            return jnp.where(sides_of[head], query[slot] * 0.125, feature_q[slot])

        def score(unit, number, rows, at, most):
            made = dot(rows, keys[unit[1], at : at + STEP], ((1,), (1,)))
            scores[number % 2, :, at : at + STEP] = made
            for lane in range(0, STEP, PAIR):
                part = made[:, lane : lane + PAIR]
                most = part if most is None else jnp.maximum(most, part)
            return most

        most, rows = None, queries(units[0])
        for at in range(0, length, STEP):
            most = score(units[0], 0, rows, at, most)
        done = {}
        for number, (slot, head) in enumerate(units):
            top = jnp.max(most, axis=1, keepdims=True)
            following = units[number + 1] if number + 1 < len(units) else None
            most, acc = None, 0.0
            if following:
                rows = queries(following)
            for at in range(0, length, STEP):
                if following:
                    most = score(following, number + 1, rows, at, most)
                weights = jnp.exp(scores[number % 2, :, at : at + STEP] - top).astype(BF16)
                acc = acc + dot(weights, values[head, at : at + STEP])
            lane = docs + (HEAD_DIM if head == 0 else 0)
            weight = acc[:, lane : lane + 1]
            done[head] = (acc / weight, top + jnp.log(weight))
            if head == heads - 1:
                result, sums = done[0]
                sums = jnp.broadcast_to(sums, (ROWS, PAIR))
                if heads > 1:
                    result = jnp.where(left, result, done[1][0])
                    sums = jnp.where(left, sums, done[1][1])
                wide[slot] = result
                total[slot] = sums
                lows[slot][...] = result.astype(BF16)

    for_heads(odd, body)


def tile_spec(array, base=0):
    lead = array.shape[:-1]
    return pl.BlockSpec(lead + (PAIR,), lambda tile: (0,) * len(lead) + (tile + base,))


def fixed_spec(array):
    return pl.BlockSpec(array.shape, lambda tile: (0,) * array.ndim)


def attend(query, keyvals, feature_q, feature_k, docs):
    slots, tiles = query.shape[0], query.shape[-1] // PAIR
    wide = jax.ShapeDtypeStruct(query.shape, F32)
    low = jax.ShapeDtypeStruct(wide.shape[1:], BF16)
    length = feature_k.shape[0] * ROWS
    made = call(
        functools.partial(attend_kernel, len(keyvals), docs, slots > 1),
        "attend",
        12,
        grid=(tiles,),
        out_shape=(wide, wide) + (low,) * slots,
        in_specs=[tile_spec(query), fixed_spec(feature_q), fixed_spec(feature_k)]
        + [tile_spec(a) for a in keyvals],
        out_specs=(tile_spec(wide),) * 2 + (tile_spec(low),) * slots,
        scratch_shapes=[
            pltpu.VMEM((2, length, PAIR), BF16),
            pltpu.VMEM((2, length, PAIR), BF16),
            pltpu.VMEM((2, ROWS, length), F32),
        ],
    )(query, feature_q, feature_k, *keyvals)
    return made[0], made[1], list(made[2:])


def attend_back_kernel(sides, docs, heads, *refs):
    query, wide, total, feature_q, feature_k = refs[:5]
    slots, length = feature_q.shape[0], feature_k.shape[0] * ROWS
    grads_in, keyvals = refs[5 : 5 + slots], refs[5 + slots : 5 + slots + sides]
    rest = refs[5 + slots + sides :]
    grad_q, outs = rest[0], rest[1 : 1 + sides]
    keys, values, queries_t, grads_t, query_own, grad_own, softs, slopes, acc = rest[1 + sides :]
    left = left_half((ROWS, PAIR))
    sides_of = (left, jnp.logical_not(left))
    zero = jnp.zeros((ROWS, PAIR), BF16)
    for head in range(heads):
        fill_keys(keyvals, feature_k, keys.at[head], values.at[head], sides_of[head])
    units = [(slot, head) for head in range(heads) for slot in range(slots)]
    for unit, (slot, head) in enumerate(units):
        mine, at = sides_of[head], head * HEAD_DIM
        rows, grads = query[slot] * 0.125, grads_in[slot][...]
        product = jnp.where(mine, grads.astype(F32) * wide[slot], 0.0)
        delta = jnp.sum(product, axis=1, keepdims=True)
        sums = total[slot, :, at : at + 1]
        spare = feature_q[slot].astype(F32) + spread3(-sums, docs, (ROWS, PAIR))
        queries_t[unit] = turn(jnp.where(mine, rows, spare.astype(BF16)))
        spare = spread3(-delta, docs, (ROWS, PAIR)).astype(BF16)
        grads_t[unit] = turn(jnp.where(mine, grads, spare))
        line = slice(unit * ROWS, (unit + 1) * ROWS)
        query_own[line] = jnp.where(mine, rows, zero)
        grad_own[line] = jnp.where(mine, grads, zero)
    per = slots * ROWS
    pieces = [(ref, index) for ref in keyvals for index in range(ref.shape[1])]
    places = [(ref, index) for ref in outs for index in range(ref.shape[1])]
    for step, at in enumerate(range(0, length, STEP)):
        which = step % 2
        for unit, (slot, head) in enumerate(units):
            line = slice(unit * ROWS, (unit + 1) * ROWS)
            soft = jnp.exp(dot(keys[head, at : at + STEP], queries_t[unit]))
            change = dot(values[head, at : at + STEP], grads_t[unit])
            softs[which, :, line] = soft.astype(BF16)
            slopes[which, :, line] = (soft * change).astype(BF16)
        out_v = dot(softs[which], grad_own[...])
        out_k = dot(slopes[which], query_own[...])
        first = at // ROWS
        for k in range(STEP // ROWS):
            ref, index = places[first + k]
            ref[0, index] = out_k[k * ROWS : (k + 1) * ROWS].astype(BF16)
            ref[1, index] = out_v[k * ROWS : (k + 1) * ROWS].astype(BF16)
        key = jnp.concatenate(
            [pieces[first + k][0][0, pieces[first + k][1]] for k in range(STEP // ROWS)], axis=0
        )
        key_t = turn(key)
        for head in range(heads):
            part = slice(head * HEAD_DIM, (head + 1) * HEAD_DIM)
            made = dot(key_t[part], slopes[which, :, head * per : (head + 1) * per])
            if step == 0:
                acc[part] = made
            else:
                acc[part] += made
    if heads == 1:
        acc[HEAD_DIM:] = jnp.zeros((PAIR - HEAD_DIM, per), F32)
    for slot in range(slots):
        made = (acc[:, slot * ROWS : (slot + 1) * ROWS] * 0.125).astype(BF16)
        grad_q[slot] = turn(made)


def attend_back(query, keyvals, grads, wide, total, feature_q, feature_k, docs, base, tiles, single):
    slots, heads = query.shape[0], 1 if single else 2
    length = feature_k.shape[0] * ROWS
    outs = tuple(
        jax.ShapeDtypeStruct(a.shape[:-1] + (tiles * PAIR,), BF16) for a in (query, *keyvals)
    )
    units = slots * heads
    made = call(
        functools.partial(attend_back_kernel, len(keyvals), docs, heads),
        "attend_back",
        8 if single else 15,
        grid=(tiles,),
        out_shape=outs,
        in_specs=[tile_spec(a, base) for a in (query, wide, total)]
        + [fixed_spec(feature_q), fixed_spec(feature_k)]
        + [tile_spec(a, base) for a in (*grads, *keyvals)],
        out_specs=tuple(tile_spec(a) for a in outs),
        scratch_shapes=[
            pltpu.VMEM((heads, length, PAIR), BF16),
            pltpu.VMEM((heads, length, PAIR), BF16),
            pltpu.VMEM((units, PAIR, ROWS), BF16),
            pltpu.VMEM((units, PAIR, ROWS), BF16),
            pltpu.VMEM((units * ROWS, PAIR), BF16),
            pltpu.VMEM((units * ROWS, PAIR), BF16),
            pltpu.VMEM((2, STEP, units * ROWS), BF16),
            pltpu.VMEM((2, STEP, units * ROWS), BF16),
            pltpu.VMEM((PAIR, slots * ROWS), F32),
        ],
    )(query, wide, total, feature_q, feature_k, *grads, *keyvals)
    return made[0], list(made[1:])


def normalise(value):
    centred = value - jnp.mean(value, axis=-1, keepdims=True)
    inverse = lax.rsqrt(jnp.mean(centred * centred, axis=-1, keepdims=True) + EPSILON)
    return centred * inverse, inverse


def norm_back(grad, gain, unit, inverse):
    scaled = grad * gain
    return inverse * (
        scaled
        - jnp.mean(scaled, axis=-1, keepdims=True)
        - unit * jnp.mean(scaled * unit, axis=-1, keepdims=True)
    )


def erf(value):
    value = jnp.clip(value, -3.7439211627767994, 3.7439211627767994)
    square = value * value
    top = 0.00022905065861350646
    for factor in (0.0034082910107109506, 0.050955695062380861, 0.18520832239976145, 1.128379143519084):
        top = top * square + factor
    bottom = -1.1791602954361697e-7
    for factor in (
        0.000023547966471313185, 0.0010179625278914885, 0.014070470171167667,
        0.11098505178285362, 0.49746925110067538, 1.0,
    ):
        bottom = bottom * square + factor
    return value * top / bottom


def column_sum(value):
    return jnp.sum(value, axis=0, keepdims=True)


def early_copies(places, blocks, weights, sems):
    if len(blocks) == 1:
        return [block_copies(places, 1, blocks, weights, sems)] + [[]] * 4
    rows = D // len(blocks)
    copies = []
    for piece in range(5):
        copies.append([])
        for slot, ref in enumerate(blocks):
            first = pl.multiple_of(places[1, slot] * rows, rows)
            copies[piece].append(
                pltpu.make_async_copy(
                    ref.at[piece * rows : (piece + 1) * rows],
                    weights.at[piece, pl.ds(first, rows), :],
                    sems.at[5 * slot + piece],
                )
            )
    return copies


def start_all(groups):
    for copies in groups:
        start(copies)


def late_rows(places, blocks, down, sems):
    rows = FF // len(blocks)
    found = []
    for slot, ref in enumerate(blocks):
        part = slice(slot * rows, (slot + 1) * rows)
        copy = pltpu.make_async_copy(ref.at[:rows], down.at[part], sems.at[slot])
        copy.start()
        found.append((pl.multiple_of(places[2, slot] * rows, rows), part, copy))
    return found


def fill_table(places, smalls, table):
    count, share = smalls.shape[0], D // smalls.shape[0]
    line = lax.broadcasted_iota(jnp.int32, (PAIR, D), 0)
    lane = lax.broadcasted_iota(jnp.int32, (PAIR, D), 1)
    made = 0.0
    for slot in range(count):
        spread = jnp.where(jnp.logical_and(lane == line + places[1, slot] * share, line < share), 1.0, 0.0)
        made = made + dot(smalls[slot, :, :PAIR], spread.astype(BF16))
    table[0:UP_B] = made[0:UP_B]
    for slot in range(count):
        at = places[1, slot]
        table[pl.ds(UP_B + at // 2, 1), pl.ds(pl.multiple_of(at % 2 * 4 * share, 4 * share), 4 * share)] = (
            smalls[slot, UP_B : UP_B + 1, : 4 * share].astype(F32)
        )


def first_kernel(count, slots, groups, places, *refs):
    blocks, refs = refs[:count], refs[count:]
    attended, refs = refs[: slots * groups], refs[slots * groups :]
    tokens, given, refs = refs[0], refs[1] if count == 1 else None, refs[1 if count > 1 else 2 :]
    many = 2 if slots > 1 else 1
    table, unit, inverse, active, slope_out, sides_out = *refs[:5], refs[5 : 5 + many]
    slope, sides = refs[5 + many], refs[6 + many : 6 + 2 * many]
    weights, turned, smalls, sems, small_sems, out_sems = refs[-6:]
    sent = []

    def leave_part(source, target):
        copy = pltpu.make_async_copy(source, target, out_sems.at[len(sent)])
        copy.start()
        sent.append(copy)

    copies = early_copies(places, blocks, weights, sems)
    if count > 1:
        start_all(copies)
        more = start(
            [
                pltpu.make_async_copy(ref.at[5 * D // count :], smalls.at[slot], small_sems.at[slot])
                for slot, ref in enumerate(blocks)
            ]
        )
    width = D // slots

    def row(at):
        return table[at : at + 1]

    core = places[0, 0] % 2 if slots > 1 else 0
    per = width // 2 if slots > 1 else width
    rows_of = [
        jnp.concatenate([a[...] for a in attended[s * groups : (s + 1) * groups]], axis=1)
        for s in range(slots)
    ]
    far = 4 * FF // 8

    for s in range(slots):
        turn_wide(rows_of[s].astype(BF16), turned)
        if slots > 1:
            first = far + (slots + s) * per
            sides[0][first : first + per] = turned[pl.ds(pl.multiple_of(core * per, per), per)]
            sides[1][first : first + per] = turned[pl.ds(pl.multiple_of((1 - core) * per, per), per)]
        else:
            sides[0][FF + D :] = turned[...]
    if count > 1:
        wait(more)
        fill_table(places, smalls, table)
    else:
        table[...] = given[...]
    wait(copies[0])
    residual = tokens[...].astype(F32) + row(PROJ_B)
    for s in range(slots):
        first = pl.multiple_of((places[0, s] // 2) * width, width)
        residual = residual + dot(rows_of[s][:, :width], weights[0, pl.ds(first, width), :])
    first_unit, first_inverse = normalise(residual)
    unit[...] = first_unit
    inverse[...] = first_inverse
    normed = first_unit * row(NORM_G) + row(NORM_S)
    normed_low = normed.astype(BF16)
    turn_wide(normed_low, turned)
    for side, target in enumerate(sides):
        if slots == 1:
            target[FF : FF + D] = turned[...]
            continue
        for s in range(slots):
            first = pl.multiple_of(places[0, side * slots + s] * per, per)
            target[far + s * per : far + (s + 1) * per] = turned[pl.ds(first, per)]
    for side, target in enumerate(sides):
        rows = slice(FF // len(sides), None)
        leave_part(target.at[rows], sides_out[side].at[rows])
    step = 384
    for at in range(0, FF, step):
        line, col = at // D, at % D
        if col == 0:
            wait(copies[1 + line])
        upward = (
            dot(normed_low, weights[1 + line, :, col : col + step])
            + table[UP_B + line : UP_B + line + 1, col : col + step]
        )
        share = 0.5 + 0.5 * erf(upward * 0.7071067811865476)
        bell = jnp.exp(upward * upward * -0.5) * 0.3989422804014327
        active[:, at : at + step] = (upward * share).astype(BF16)
        slope[:, at : at + step] = (share + upward * bell).astype(BF16)
        if (at + step) % D == 0:
            lanes = slice(at + step - D, at + step)
            leave_part(slope.at[:, lanes], slope_out.at[:, lanes])
    for side, target in enumerate(sides):
        if slots == 1:
            turn_wide(active, target)
            leave_part(target.at[:FF], sides_out[side].at[:FF])
            continue
        rows = FF // 8
        for s in range(slots):
            first = pl.multiple_of(places[0, side * slots + s] * rows, rows)
            for at in range(0, rows, PAIR):
                block = active[:, pl.ds(pl.multiple_of(first + at, PAIR), PAIR)]
                target[s * rows + at : s * rows + at + PAIR] = turn(block)
            part = slice(s * rows, (s + 1) * rows)
            leave_part(target.at[part], sides_out[side].at[part])
    wait(sent)


def first_part(places, blocks, attended, tokens, table):
    count = len(blocks)
    slots = 4 if count > 1 else 1
    groups = len(attended) // slots
    given = [table] if count == 1 else []
    shape = jax.ShapeDtypeStruct
    sides = 2 if slots > 1 else 1
    outs = (
        shape((TABLE, D), F32), shape((ROWS, D), F32), shape((ROWS, 1), F32),
        shape((ROWS, FF), BF16), shape((ROWS, FF), BF16),
    )
    outs += (shape(((FF + 2 * D) // sides, ROWS), BF16),) * sides
    made = call(
        functools.partial(first_kernel, count, slots, groups),
        "forward_up",
        11,
        out_shape=outs,
        in_specs=[SMEM] + [ANY] * count + [VMEM] * (slots * groups + 1 + len(given)),
        out_specs=(VMEM,) * 4 + (ANY,) * (1 + sides),
        scratch_shapes=like(outs[4:])
        + [
            pltpu.VMEM((5, D, D), BF16),
            pltpu.VMEM((D, ROWS), BF16),
            pltpu.VMEM((count, TABLE, D), BF16),
            pltpu.SemaphoreType.DMA((5 * count,)),
            pltpu.SemaphoreType.DMA((count,)),
            pltpu.SemaphoreType.DMA((16,)),
        ],
    )(places, *blocks, *attended, tokens, *given)
    return made[:5], made[5:]


def head_kernel(count, docs, places, *refs):
    blocks, refs = refs[:count], refs[count:]
    unit, active, cotangent, table, numbers = refs[:5]
    output, lines, docs_out, grad_second, grad_out = refs[5:10]
    pool, down, sems = refs[10:]
    down_parts = late_rows(places, blocks, down, sems.at[1])
    pool_copies = block_copies(places, 2, blocks, pool, sems.at[0], slice(FF // count, (FF + D) // count))

    def row(at):
        return table[at : at + 1]

    normed = unit[...] * row(NORM_G) + row(NORM_S)
    residual = normed + row(DOWN_B)
    for first, part, copy in down_parts:
        copy.wait()
        residual = residual + dot(active[:, pl.ds(first, FF // count)], down[part])
    last_unit, last_inverse = normalise(residual)
    outcome = last_unit * row(FINAL_G) + row(FINAL_S)
    out_low = outcome.astype(BF16)
    output[...] = out_low

    at_row, label = numbers[:, 0:1], numbers[:, 1:2]
    here = jnp.logical_and(at_row >= 0.0, at_row < float(ROWS))
    line = lax.broadcasted_iota(jnp.int32, (docs, ROWS), 1).astype(F32)
    pick = jnp.where(line == at_row, 1.0, 0.0)
    first_low = dot(pick.astype(BF16), out_low).astype(BF16)
    wait(pool_copies)
    pooled = jnp.tanh(dot(first_low, pool[...]) + row(POOL_B))
    pooled_low = pooled.astype(BF16).astype(F32)
    logits = [
        jnp.sum(pooled_low * row(CLASS_W + c), axis=1, keepdims=True)
        + numbers[:, 2 + c : 3 + c]
        for c in range(CLASSES)
    ]
    top = functools.reduce(jnp.maximum, logits)
    powers = [jnp.exp(logit - top) for logit in logits]
    whole = functools.reduce(jnp.add, powers)
    grads = [powers[c] / whole - jnp.where(label == float(c), 1.0, 0.0) for c in range(CLASSES)]
    grad_pre = functools.reduce(jnp.add, [grads[c] * row(CLASS_W + c) for c in range(CLASSES)])
    grad_pre = grad_pre * (1.0 - pooled * pooled)
    parts = jnp.concatenate(split3(grad_pre), axis=0).astype(BF16)
    made = dot(parts, pool[...], ((1,), (1,)))
    grad_first = made[:docs] + made[docs : 2 * docs] + made[2 * docs :]
    parts = jnp.concatenate(split3(grad_first), axis=0).astype(BF16)
    picks = jnp.concatenate([pick] * 3, axis=0).astype(BF16)
    grad_outcome = cotangent[...] + dot(picks, parts, ((0,), (0,)))
    lane = lax.broadcasted_iota(jnp.int32, (docs, 128), 1)
    small = jnp.zeros((docs, 128), F32)
    for c in range(CLASSES):
        small = jnp.where(lane == c, grads[c], jnp.where(lane == CLASSES + c, logits[c], small))
    docs_out[...] = jnp.where(
        here,
        jnp.concatenate([first_low.astype(F32), pooled_low, grad_pre, small], axis=1),
        0.0,
    )

    grad = norm_back(grad_outcome, row(FINAL_G), last_unit, last_inverse)
    grad_second[...] = grad
    grad_out[...] = grad.astype(BF16)
    lines[0:1] = column_sum(grad)
    lines[1:2] = column_sum(grad_outcome * last_unit)
    lines[2:3] = column_sum(grad_outcome)
    lines[3:8] = jnp.zeros((5, D), F32)


def head_part(places, late, unit, active, cotangent, table, numbers):
    count, docs = len(late), numbers.shape[0]
    shape = jax.ShapeDtypeStruct
    outs = (
        shape((ROWS, D), BF16),
        shape((8, D), F32),
        shape((docs, 3 * D + 128), F32),
        shape((ROWS, D), F32),
        shape((ROWS, D), BF16),
    )
    return call(
        functools.partial(head_kernel, count, docs),
        "head",
        7,
        out_shape=outs,
        in_specs=[SMEM] + [ANY] * count + [VMEM] * 5,
        out_specs=(VMEM,) * len(outs),
        scratch_shapes=[
            pltpu.VMEM((D, D), BF16),
            pltpu.VMEM((FF, D), BF16),
            pltpu.SemaphoreType.DMA((2, count)),
        ],
    )(places, *late, unit, active, cotangent, table, numbers)


def second_kernel(count, places, *refs):
    downs, (grad_down, slope, lines, grad_up, down, sems) = refs[:count], refs[count:]
    grad_low = grad_down[...]
    whole = FF // count
    step = min(whole, 384)
    for first, part, copy in late_rows(places, downs, down, sems):
        copy.wait()
        for at in range(0, whole, step):
            rows = down[part.start + at : part.start + at + step]
            grad = dot(grad_low, rows, ((1,), (1,))).astype(BF16).astype(F32)
            here = pl.multiple_of(first + at, step)
            grad = grad * slope[:, pl.ds(here, step)].astype(F32)
            line, col = here // D, pl.multiple_of(here % D, step)
            lines[pl.ds(line, 1), pl.ds(col, step)] = column_sum(grad)
            grad_up[line, :, pl.ds(col, step)] = grad.astype(BF16)
    lines[4:8] = jnp.zeros((4, D), F32)


def second_part(places, late, grad_down, slope):
    count, shape = len(late), jax.ShapeDtypeStruct
    outs = (shape((8, D), F32), shape((4, ROWS, D), BF16))
    return call(
        functools.partial(second_kernel, count),
        "backward_down",
        5,
        out_shape=outs,
        in_specs=[SMEM] + [ANY] * count + [VMEM] * 2,
        out_specs=(VMEM,) * 2,
        scratch_shapes=[pltpu.VMEM((FF, D), BF16), pltpu.SemaphoreType.DMA((count,))],
    )(places, *late, grad_down, slope)


def third_kernel(count, slots, places, *refs):
    blocks, refs = refs[:count], refs[count:]
    table, grad_second, grad_up, unit, inverse = refs[:5]
    lines, grad_first, grad_out = refs[5:8]
    grad_attended = refs[8 : 8 + slots]
    weights, sems = refs[8 + slots :]
    copies = early_copies(places, blocks, weights, sems)
    if count > 1:
        start_all(copies[1:] + copies[:1])
    else:
        wait(copies[0])
    width = D // slots

    def row(at):
        return table[at : at + 1]

    back = 0.0
    for line in range(4):
        wait(copies[1 + line])
        back = back + dot(grad_up[line], weights[1 + line], ((1,), (1,)))
    grad_normed = grad_second[...] + back.astype(BF16).astype(F32)
    lines[0:4] = jnp.zeros((4, D), F32)
    lines[4:5] = column_sum(grad_normed * unit[...])
    lines[5:6] = column_sum(grad_normed)
    grad = norm_back(grad_normed, row(NORM_G), unit[...], inverse[...])
    grad_first[...] = grad
    lines[6:7] = column_sum(grad)
    lines[7:8] = jnp.zeros((1, D), F32)
    grad_low = grad.astype(BF16)
    grad_out[...] = grad_low
    if count > 1:
        wait(copies[0])
    for s in range(slots):
        first = pl.multiple_of((places[0, s] // 2) * width, width)
        made = dot(grad_low, weights[0, pl.ds(first, width), :], ((1,), (1,))).astype(BF16)
        if width < grad_attended[s].shape[1]:
            grad_attended[s][:, PAIR:] = jnp.zeros((ROWS, PAIR), BF16)
        grad_attended[s][:, :width] = made


def third_part(places, blocks, table, grad_second, grad_up, unit, inverse, slots, lanes):
    count = len(blocks)
    shape = jax.ShapeDtypeStruct
    outs = (shape((8, D), F32), shape((ROWS, D), F32), shape((ROWS, D), BF16))
    outs += (shape((ROWS, lanes), BF16),) * slots
    made = call(
        functools.partial(third_kernel, count, slots),
        "backward_up",
        7,
        out_shape=outs,
        in_specs=[SMEM] + [ANY] * count + [VMEM] * 5,
        out_specs=(VMEM,) * len(outs),
        scratch_shapes=[pltpu.VMEM((5, D, D), BF16), pltpu.SemaphoreType.DMA((5 * count,))],
    )(places, *blocks, table, grad_second, grad_up, unit, inverse)
    return made[:3], list(made[3:])


def wgrad_outs(slots, rows):
    shape = jax.ShapeDtypeStruct
    if slots == 1:
        return (shape((1, rows, D), BF16),)
    half = rows // 2
    return (shape((2, half, D), BF16),) * 2 + (shape((half, D), BF16),) * 2 + (shape((rows, D), F32),)


def put_slot(outs, s, first, value):
    if len(outs) == 1:
        outs[0][0, first : first + value.shape[0]] = value.astype(BF16)
        return
    if s == 0:
        outs[4][first : first + value.shape[0]] = value
        return
    half = outs[2].shape[0]
    for k, order in enumerate(((1, 3, 2), (2, 3, 1))):
        low, high = max(first, k * half), min(first + value.shape[0], (k + 1) * half)
        if low >= high:
            continue
        rows, part = slice(low - k * half, high - k * half), value[low - first : high - first]
        if s == order[2]:
            outs[2 + k][rows] = part.astype(BF16)
        else:
            outs[k][order.index(s), rows] = part.astype(BF16)


def gradient_call(body, name, micros, ins, outs, scratch, waits):
    return call(
        body,
        name,
        micros,
        out_shape=outs,
        in_specs=[ANY] * len(ins),
        out_specs=(ANY,) * len(outs),
        scratch_shapes=[pltpu.VMEM(a.shape, a.dtype) for a in outs]
        + scratch
        + [pltpu.SemaphoreType.DMA((waits,)), pltpu.SemaphoreType.DMA((len(outs),))],
    )(*ins)


def leave(kept, outs, sems, which):
    return start([pltpu.make_async_copy(kept[k], outs[k], sems.at[k]) for k in which])


def down_kernel(slots, sides, *refs):
    lefts, rights, refs = refs[:sides], refs[sides : 2 * sides], refs[2 * sides :]
    count = 5 if slots > 1 else 1
    outs, kept, (left, right, sems, out_sems) = refs[:count], refs[count : 2 * count], refs[-4:]
    rows = FF // sides // slots
    step = min(rows, 384)
    copies = {}
    for side in range(sides):
        copies[side] = pltpu.make_async_copy(rights[side], right.at[side], sems.at[side])
    order = (3, 1, 2, 0) if slots > 1 else (0,)
    for s in order:
        for side in range(sides):
            part = slice(s * rows, (s + 1) * rows)
            copies[s, side] = pltpu.make_async_copy(
                lefts[side].at[part], left.at[side, part], sems.at[sides + s * sides + side]
            )
    start(copies.values())
    wait([copies[side] for side in range(sides)])
    sent = []
    for s in order:
        wait([copies[s, side] for side in range(sides)])
        for at in range(0, rows, step):
            first = s * rows + at
            made = dot(left[0, first : first + step], right[0])
            for side in range(1, sides):
                made = made + dot(left[side, first : first + step], right[side])
            put_slot(kept, s, at, made)
        if slots > 1:
            sent += leave(kept, outs, out_sems, {3: (), 1: (0, 3), 2: (1, 2), 0: (4,)}[s])
        else:
            sent += leave(kept, outs, out_sems, (0,))
    wait(sent)


def down_gradient(lefts, rights, slots):
    sides = len(lefts)
    outs = wgrad_outs(slots, FF // sides // slots)
    scratch = [pltpu.VMEM((sides, FF // sides, ROWS), BF16), pltpu.VMEM((sides, ROWS, D), BF16)]
    body = functools.partial(down_kernel, slots, sides)
    return gradient_call(
        body, "down_gradient", 3, (*lefts, *rights), outs, scratch, sides * (slots + 1)
    )


def up_kernel(slots, sides, *refs):
    lefts, ups, projs, refs = *(refs[k * sides : (k + 1) * sides] for k in range(3)), refs[3 * sides :]
    count = 5 if slots > 1 else 1
    outs, kept, (left, right, sems, out_sems) = refs[:count], refs[count : 2 * count], refs[-4:]
    whole = D // sides
    rows = whole // slots
    copies = {}
    for side in range(sides):
        copies[side] = pltpu.make_async_copy(
            lefts[side].at[FF // sides :], left.at[side], sems.at[side]
        )
    for line in range(5):
        for side in range(sides):
            copies[line, side] = pltpu.make_async_copy(
                ups[side].at[line] if line < 4 else projs[side],
                right.at[side, line],
                sems.at[sides + line * sides + side],
            )
    start(copies.values())
    wait([copies[side] for side in range(sides)])
    sent = []
    for line in range(5):
        wait([copies[line, side] for side in range(sides)])
        at = 0 if line < 4 else whole
        made = dot(left[0, at : at + whole], right[0, line])
        for side in range(1, sides):
            made = made + dot(left[side, at : at + whole], right[side, line])
        for s in range(slots):
            put_slot(kept, s, line * rows, made[s * rows : (s + 1) * rows])
        if slots > 1:
            sent += leave(kept, outs, out_sems, {2: (0, 2), 4: (1, 3, 4)}.get(line, ()))
        elif line == 4:
            sent += leave(kept, outs, out_sems, (0,))
    wait(sent)


def up_gradient(lefts, ups, projs, slots):
    sides = len(lefts)
    outs = wgrad_outs(slots, 5 * D // sides // slots)
    scratch = [pltpu.VMEM((sides, 2 * D // sides, ROWS), BF16), pltpu.VMEM((sides, 5, ROWS, D), BF16)]
    body = functools.partial(up_kernel, slots, sides)
    return gradient_call(body, "up_gradient", 4, (*lefts, *ups, *projs), outs, scratch, 6 * sides)


def input_kernel(groups, sides, places, *refs):
    turned, refs = refs[:sides], refs[sides:]
    grad_qs, refs = refs[:groups], refs[groups:]
    changes, refs = refs[: groups * sides], refs[groups * sides :]
    outs, (made, lines, grads, sems) = refs[:-4], refs[-4:]
    rows = turned[0].shape[1]
    count = outs[0].shape[0] // 3 // (D // (8 if sides > 1 else 1))
    share = D // (8 if sides > 1 else 1)
    sums, sends = [], []
    for k in range(3):
        total, line = None, None
        for side in range(sides if k else 1):
            lane = 0
            for group in range(groups):
                source = changes[group * sides + side].at[k - 1] if k else grad_qs[group]
                lanes = slice(lane, lane + source.shape[2])
                lane = lanes.stop
                grads[:, lanes] = source[...].reshape(rows, source.shape[2])
            part = dot(turned[side][...], grads[...])
            total = part if total is None else total + part
            if k != 1:
                part = dot(jnp.ones((8, rows), BF16), grads[...])
                line = part if line is None else line + part
        made[k] = total.astype(BF16)
        if k != 1:
            sums.append(line[:1])
        for side, out in enumerate(outs):
            for s in range(count):
                first = pl.multiple_of(places[0, side * count + s] * share, share)
                target = out.at[(3 * s + k) * share : (3 * s + k + 1) * share]
                sends.append((made.at[k, pl.ds(first, share), :], target))
                pltpu.make_async_copy(*sends[-1], sems.at[len(sends) - 1]).start()
    lines[...] = jnp.concatenate([*sums, jnp.zeros((14, lines.shape[1]), F32)], axis=0).astype(BF16)
    for out in outs:
        sends.append((lines, out.at[3 * count * share :]))
        pltpu.make_async_copy(*sends[-1], sems.at[len(sends) - 1]).start()
    wait([pltpu.make_async_copy(a, b, sems.at[k]) for k, (a, b) in enumerate(sends)])


def input_gradient(places, turned, grad_qs, changes, slots):
    lanes = sum(grad.shape[2] for grad in grad_qs)
    sides, groups = len(turned), len(grad_qs)
    out = jax.ShapeDtypeStruct((3 * D // sides + 16, lanes), BF16)
    made = call(
        functools.partial(input_kernel, groups, sides),
        "input_weights",
        5,
        out_shape=(out,) * sides,
        in_specs=[SMEM] + [VMEM] * (sides + groups + groups * sides),
        out_specs=(ANY,) * sides,
        scratch_shapes=[
            pltpu.VMEM((3, D, lanes), BF16),
            pltpu.VMEM((16, lanes), BF16),
            pltpu.VMEM((turned[0].shape[1], lanes), BF16),
            pltpu.SemaphoreType.DMA((sides * (3 * slots + 1),)),
        ],
    )(places, *turned, *grad_qs, *changes)
    return list(made)


def last_kernel(sides, groups, parts, places, *refs):
    weights, refs = refs[:sides], refs[sides:]
    grad_qs, refs = refs[:groups], refs[groups:]
    changes, refs = refs[: groups * parts], refs[groups * parts :]
    grad_first, own, outs = *refs[:2], refs[2:-3]
    held, grads, sems = refs[-3:]
    slots = grad_qs[0].shape[0]
    copies = block_copies(places, 0, weight_refs(weights), held, sems)
    for s in range(slots):
        rows = slice(s * ROWS, (s + 1) * ROWS)
        lane = 0
        for group in range(groups):
            lanes = slice(lane, lane + grad_qs[group].shape[2])
            lane = lanes.stop
            grads[0, rows, lanes] = grad_qs[group][s]
            for k in range(2):
                total = changes[group * parts][k, s].astype(F32)
                for change in changes[group * parts + 1 : (group + 1) * parts]:
                    total = total + change[k, s].astype(F32)
                grads[1 + k, rows, lanes] = total.astype(BF16)
    wait(copies)

    def partial(s):
        rows = slice(s * ROWS, (s + 1) * ROWS)
        total = dot(grads[0, rows], held[0], ((1,), (1,)))
        for k in range(1, 3):
            total = total + dot(grads[k, rows], held[k], ((1,), (1,)))
        return total

    for s in range(1, slots):
        outs[s - 1][...] = partial(s).astype(BF16)
    own[...] = grad_first[...] + partial(0)


def last_part(places, weights, grad_qs, changes, grad_first):
    slots, lanes = grad_qs[0].shape[0], sum(grad.shape[2] for grad in grad_qs)
    groups, parts = len(grad_qs), len(changes) // len(grad_qs)
    sides, shape = len(weights), jax.ShapeDtypeStruct
    outs = (shape((ROWS, D), F32),) + (shape((ROWS, D), BF16),) * (slots - 1)
    blocks = sides * weights[0].shape[0]
    made = call(
        functools.partial(last_kernel, sides, groups, parts),
        "input_gradients",
        5,
        out_shape=outs,
        in_specs=[SMEM] + [ANY] * sides + [VMEM] * (1 + groups + len(changes)),
        out_specs=(VMEM,) * len(outs),
        scratch_shapes=[
            pltpu.VMEM((3, D, lanes), BF16),
            pltpu.VMEM((3, slots * ROWS, lanes), BF16),
            pltpu.SemaphoreType.DMA((blocks,)),
        ],
    )(places, *weights, *grad_qs, *changes, grad_first)
    return made[0], made[1:]


def whole_scatter(part, pieces):
    seq = lax.axis_size("seq")
    rows = part.shape[1] // pieces // seq
    part = part.reshape(pieces, seq, rows, D).transpose(1, 0, 2, 3)
    part = part.reshape(seq, pieces * rows, D)
    return lax.psum_scatter(part, "seq", scatter_dimension=0, tiled=True)[0].astype(F32)


def by_chip(pieces):
    me = lax.axis_index("seq")
    for bit in (1, 2):
        odd = (me & (2 * bit)) != 0
        pieces = [jnp.where(odd, pieces[s ^ bit], pieces[s]) for s in range(len(pieces))]
    return pieces


def features(positions, starts):
    docs = starts.shape[0]
    segment = jnp.sum((positions[..., None] >= starts).astype(jnp.int32), axis=-1) - 1
    lane = jnp.arange(PAIR, dtype=jnp.int32) % HEAD_DIM
    own = segment[..., None] == lane
    return own, lane, docs


def on_device(
    inputs,
    cotangent,
    doc_lengths,
    doc_labels,
    query_weight,
    query_bias,
    key_weight,
    value_weight,
    value_bias,
    proj_weight,
    proj_bias,
    norm_gain,
    norm_shift,
    up_weight,
    up_bias,
    down_weight,
    down_bias,
    final_gain,
    final_shift,
    pool_weight,
    pool_bias,
    class_weight,
    class_bias,
):
    me = lax.axis_index("seq")
    tokens = inputs[0]
    share = query_bias.shape[0]
    lengths = doc_lengths[0]
    docs = lengths.shape[0]
    order = jnp.arange(docs, dtype=jnp.int32)
    starts = jnp.sum(jnp.where(order[None, :] < order[:, None], lengths[None, :], 0), axis=1)

    numbers = jnp.concatenate(
        [
            (starts - me * ROWS)[:, None].astype(F32),
            doc_labels[0][:, None].astype(F32),
            jnp.broadcast_to(class_bias.astype(F32), (docs, CLASSES)),
            jnp.zeros((docs, PAIR - 2 - CLASSES), F32),
        ],
        axis=1,
    )

    small_mesh = is_small()
    slot_list = slot_owners()
    chip, core = me // 2, me % 2
    width = D // 4
    slots = 4 if small_mesh else 1
    line = jnp.arange(ROWS, dtype=jnp.int32)
    mine = slot_list[:slots] if small_mesh else me[None]
    own, lane, _ = features(mine[:, None] * ROWS + line, starts)
    feature_q = jnp.where(own, FAR, 0.0).astype(BF16)
    own, lane, _ = features(slot_list[:, None] * ROWS + line, starts)
    feature_k = jnp.where(
        lane < docs, jnp.where(own, 0.0, 1.0), jnp.where(lane < docs + 3, 1.0, 0.0)
    ).astype(BF16)

    matrices = jnp.stack([query_weight, key_weight, value_weight])
    bias = jnp.stack([query_bias, value_bias])
    small = jnp.stack(
        [
            query_bias, value_bias, proj_bias, norm_gain, norm_shift, down_bias,
            final_gain, final_shift, pool_bias, *class_weight.T,
        ]
    )
    wide = me * up_bias.shape[0]
    up_pieces = up_weight.reshape(share, 4, D).transpose(1, 0, 2)
    proj_up = jnp.concatenate([proj_weight[None], up_pieces])
    down_pool = jnp.concatenate([down_weight, pool_weight])
    if small_mesh:
        pieces = [
            lax.dynamic_slice_in_dim(matrices, (chip ^ s) * width, width, 2) for s in range(4)
        ]
        token_blocks = gather_tokens(tokens)
        own = jnp.stack(exchange(pieces))
        own = jnp.pad(own, ((0, 0), (0, 0), (0, 0), (0, PAIR * 2 - width)))
        small = jnp.pad(small, ((0, TABLE - small.shape[0]), (0, D - share)))
        small = lax.dynamic_update_slice(small, up_bias[None], (UP_B, 0))
        early = Shared(jnp.concatenate([proj_up.reshape(5 * share, D), small]), 0)
        late = Shared(down_pool, 1)
        places = jnp.stack([slot_list, early.owners(), late.owners()])
        come = swap(bias, along(1))
        bias = jnp.where(
            core == 0, jnp.concatenate([bias, come], axis=1), jnp.concatenate([come, bias], axis=1)
        )
        bias = jnp.pad(bias, ((0, 0), (0, PAIR * 2 - width))).astype(F32)
        own = after(own, feature_q, feature_k, places, bias, numbers, token_blocks[1:3])
        weights = [own, swap(own, along(1))]
        early.near()
        late.near()
        table = None
    else:
        token_blocks = [tokens]
        weights = [lax.all_gather(matrices, "seq", axis=1, tiled=True)[None]]
        table = jnp.zeros((TABLE, D), BF16)
        table = lax.dynamic_update_slice(table, small, (0, me * share))
        table = lax.dynamic_update_slice(table, up_bias[None], (UP_B + wide // D, wide % D))
        table = sum_seq(table).astype(F32)
        bias = table[:2]
        blocks = [lax.all_gather(proj_up, "seq", axis=1, tiled=True)]
        whole = lax.all_gather(down_pool, "seq", axis=0)
        whole = [whole[:, : 4 * share].reshape(FF, D), whole[:, 4 * share :].reshape(D, D)]
        late_blocks = [jnp.concatenate(whole)]
        places = jnp.zeros((3, 1), jnp.int32)

    query, keyval = qkv_project(places, token_blocks, weights, bias)
    tokens_t = turn_tokens(after(token_blocks, query))
    if small_mesh:
        early.one, late.one = after((early.one, late.one), tokens_t)
        keyval = after(keyval, early.one, late.one)
        keyvals = [keyval, swap(keyval, along(1))]
        early.far()
        early.rest()
        early.cross()
        late.far()
    else:
        keyvals = [lax.all_gather(keyval, "seq", axis=1, tiled=True)]
    attended, total, lows = attend(query, keyvals, feature_q, feature_k, docs)
    if small_mesh:
        lows, tokens_t, early.both, early.other, early.crossed = after(
            (lows, tokens_t, early.both, early.other, early.crossed), lows
        )
        early.cross_both()
        blocks = early.finish()
    else:
        tokens_t = [tokens_t]
    lows = exchange(lows)
    if small_mesh:
        late.shard, late.one, late.both = after((late.shard, late.one, late.both), lows)
        late.rest_direct()
        late.cross()
        late.cross_both()

    made, turned = first_part(places, blocks, lows, tokens, table)
    table, unit, inverse, active, slope = made
    if small_mesh:
        late.other, late.crossed, late.middle, tokens_t, turned = after(
            (late.other, late.crossed, late.middle, tokens_t, turned), active
        )
        late_blocks = late.finish()
        tokens_t = [tokens_t, swap(tokens_t, along(1))]
    output, lines_one, docs_out, grad_second, grad_down = head_part(
        places, late_blocks, unit, active, cotangent[0], table, numbers
    )

    def both(keep, *away):
        return [keep] + [swap(a, along(1)) for a in away]

    def own_and_other(value):
        return both(value, *([value] if small_mesh else []))

    turned = both(*turned)
    down_parts = down_gradient(turned, own_and_other(grad_down), slots)
    if small_mesh:
        down_sum = Scatter(down_parts)
    grad_down = after(grad_down, down_parts, tokens_t)
    lines_two, grad_up = second_part(places, late_blocks, grad_down, slope)
    grad_second = after(grad_second, grad_up)
    made, grads = third_part(
        places, blocks, table, grad_second, grad_up, unit, inverse, slots, query.shape[-1]
    )
    lines_three, grad_first, grad_proj = made
    lines_two = lines_two + lines_three
    pack = jnp.concatenate([docs_out, lines_one, lines_two], axis=1)
    ups = own_and_other(grad_up)
    if small_mesh:
        grad_proj, grads = after((grad_proj, grads), down_sum.comes)
        down_sum.combine()
        down_sum.turn()
        grads = exchange(grads)
    up_parts = up_gradient(turned, ups, own_and_other(grad_proj), slots)

    back = functools.partial(
        attend_back, keyvals=keyvals,
        feature_q=feature_q, feature_k=feature_k, docs=docs,
    )
    if small_mesh:
        up_parts, pack, grads, down_sum.lasts = after(
            (up_parts, pack, grads, down_sum.lasts), up_parts
        )
        down_dp = SumDp(down_sum.total())
        up_sum = Scatter(up_parts)
        come = swap(pack, along(1))
        grad_q, changes = back(
            query, grads=grads, wide=attended, total=total, base=0, tiles=1, single=False
        )
        changes, pack, come, up_sum.seconds, down_dp.come = after(
            (changes, pack, come, up_sum.seconds, down_dp.come), grad_q, up_sum.comes
        )
        grad_qs, partial, changes = [grad_q], list(changes), both(*changes)
        up_sum.combine()
        up_sum.turn()
        down_dp.across()
        pack = pack + come
        come = swap(pack, along(2))
        rows = after(query, grad_q, up_sum.sends, down_dp.pair, pack)
        grad_q, more = back(
            rows, grads=grads, wide=attended, total=total, base=1, tiles=1, single=True
        )
        more, pack, come, up_sum.lasts, down_dp.cross = after(
            (more, pack, come, up_sum.lasts, down_dp.cross), grad_q
        )
        grad_qs, partial = grad_qs + [grad_q], partial + list(more)
        changes = changes + both(*more)
        up_dp = SumDp(up_sum.total())
        pack = pack + come
        come = swap(pack, along(4))
    else:
        grad_q, changes = back(
            query, grads=grads, wide=attended, total=total,
            base=0, tiles=HEADS // 2, single=False,
        )
        grad_qs, partial = [grad_q], changes
        change = changes[0].transpose(1, 0, 2, 3)
        change = lax.psum_scatter(change, "seq", scatter_dimension=0, tiled=True)
        changes = [change.transpose(1, 0, 2, 3)]
        partial = changes
        pack = sum_seq(pack)
    def own_shares(pack):
        at = me * share
        lines = pack[:, 3 * D + PAIR :].reshape(docs, 2, D).transpose(1, 0, 2).reshape(2 * docs, D)
        own = jnp.concatenate(
            [
                lax.dynamic_slice_in_dim(lines, at, share, 1),
                lax.dynamic_slice_in_dim(lines[8:12].reshape(-1), wide, 4 * share, 0).reshape(4, share),
                jnp.zeros((4, share), F32),
            ]
        )
        parts = [
            pack[:, 2 * D : 3 * D],
            lax.dynamic_slice_in_dim(pack, at, share, 1),
            lax.dynamic_slice_in_dim(pack, D + at, share, 1),
            pack[:, 3 * D : 3 * D + PAIR],
            own.reshape(docs, 3 * share),
        ]
        logits = pack[:, 3 * D + CLASSES : 3 * D + 2 * CLASSES]
        return jnp.concatenate(parts, axis=1), logits

    qkv_parts = input_gradient(places, tokens_t, grad_qs, partial, slots)
    if small_mesh:
        qkv_parts, changes, pack, come, up_dp.come, down_dp.cross = after(
            (qkv_parts, changes, pack, come, up_dp.come, down_dp.cross), qkv_parts
        )
        keep, away = both(*qkv_parts)
        up_dp.across()
        away = after(away, up_dp.pair)
        rows = 3 * share
        pieces = [
            add(keep[s * rows : (s + 1) * rows, :width], away[s * rows : (s + 1) * rows, :width])
            for s in range(4)
        ]
        ends = add(keep[4 * rows : 4 * rows + 2], away[4 * rows : 4 * rows + 2])
        pieces = [piece.astype(BF16) for piece in pieces]
        pack, come = after((pack, come), pieces)
        pieces = exchange(pieces)
        pack, logits = own_shares(pack + come)
        come = swap(pack, lambda z, i: (z ^ 1, i))
        changes = after(changes, pieces[0], pack, ends)
    input_grad, sums = last_part(places, weights, grad_qs, changes, grad_first)

    if small_mesh:
        pieces, down_dp.cross, pack, come = after(
            (pieces, down_dp.cross, pack, come), input_grad
        )
        qkv_wgrad = jnp.concatenate(by_chip(pieces), axis=1)
        ends = jnp.pad(
            lax.dynamic_slice_in_dim(ends, core * share, share, 1), ((0, 30), (0, D - share))
        )
        qkv_dp = SumDp(jnp.concatenate([qkv_wgrad.astype(F32), ends]))
        pack = jnp.concatenate([pack, come], axis=0)
        come = swap(pack, lambda z, i: (z ^ 2, i))
        down_dp.finish()
        sums = exchange([input_grad, *sums])
        qkv_dp.come, up_dp.cross = after((qkv_dp.come, up_dp.cross), qkv_dp.come)
        qkv_dp.across()
        up_dp.finish()
        every_doc = jnp.concatenate([pack, come], axis=0)
        qkv_dp.cross, sums, every_doc, down_dp.last = after(
            (qkv_dp.cross, sums, every_doc, down_dp.last), qkv_dp.cross
        )
        qkv_dp.finish()
        down_wgrad, up_wgrad = down_dp.back(), up_dp.back()
        input_grad = add(*sums)
        qkv_wgrad = qkv_dp.back()
    else:
        qkv_wgrad = whole_scatter(qkv_parts[0][None, : 3 * D], 3)
        ends = sum_seq(qkv_parts[0][3 * D : 3 * D + 2].astype(F32))
        ends = lax.dynamic_slice_in_dim(ends, me * share, share, 1)
        qkv_wgrad = sum_dp(jnp.concatenate([qkv_wgrad, jnp.pad(ends, ((0, 30), (0, D - share)))]))
        down_wgrad = sum_dp(whole_scatter(down_parts[0], 1))
        up_wgrad = sum_dp(whole_scatter(up_parts[0], 5))
    proj_wgrad = up_wgrad[4 * share :]
    up_wgrad = up_wgrad[: 4 * share].reshape(4, share, D).transpose(1, 0, 2).reshape(share, FF)
    ends = qkv_wgrad[3 * share : 3 * share + 2, :share]
    qkv_wgrad = qkv_wgrad[: 3 * share].reshape(3, share, D)
    if not small_mesh:
        pack, logits = own_shares(pack)
        every_doc = stack_dp(pack)
    pre_all, first_all, pooled_all = (
        every_doc[:, at : at + size] for at, size in ((0, D), (D, share), (D + share, share))
    )
    logit_all = every_doc[:, D + 2 * share : D + 2 * share + CLASSES]
    lines = jnp.sum(every_doc[:, D + 2 * share + PAIR :].reshape(-1, docs, 3 * share), axis=0)
    lines = lines.reshape(3 * docs, share)

    def my_share(vector):
        return lax.dynamic_slice_in_dim(vector, me * share, share, 0)

    exact = functools.partial(jnp.dot, precision=lax.Precision.HIGHEST)
    return (
        output[None],
        logits[None],
        input_grad[None],
        qkv_wgrad[0],
        ends[0],
        qkv_wgrad[1],
        qkv_wgrad[2],
        ends[1],
        proj_wgrad,
        lines[14],
        lines[12],
        lines[13],
        up_wgrad,
        lines[16:20].reshape(-1),
        down_wgrad,
        lines[0],
        lines[1],
        lines[2],
        exact(first_all.T, pre_all),
        my_share(jnp.sum(pre_all, axis=0)),
        exact(pooled_all.T, logit_all),
        jnp.sum(logit_all, axis=0),
    )


def solution(mesh):
    rows, row, part = P("dp", "seq", None), P("seq", None), P("seq")
    per_sequence = P("dp", None)
    in_specs = (
        rows, rows, per_sequence, per_sequence, row, part, row, row, part, row, part, part,
        part, row, part, row, part, part, part, row, part, row, P(),
    )
    out_specs = (
        rows, P("dp", None, None), rows, row, part, row, row, part, row, part, part, part,
        row, part, row, part, part, part, row, part, row, P(),
    )
    return jax.shard_map(
        on_device, mesh=mesh, in_specs=in_specs, out_specs=out_specs, check_vma=False
    )
```

profile of v0, /device:TPU:0, one launch (start us, length us, event | category | flops | bytes accessed | tf_op | source)
XLA Modules:
  0.0 265.3 jit_solution(10460746244357640894)
XLA Ops:
  0.7 3.0 %collective-permute-start.2 = (bf16[256,768]{1,0:T(8,128)(2,1)}, bf16[256,768]{1,0:T(8,128)(2,1)S(1)}, u32[]{:S(2)}, u32[]{:S(2)}) collective-permute-start(bf16[256,768]{1,0:T(8,128)(2,1)} %bitcast.28.refs_0_.refs_12_), channel_id=1, source_target_pairs={{0,2},{1,3},{2,0},{3,1},{4,6},{5,7},{6,4},{7,5},{8,10},{9,11},{10,... | collective-permute-start | bytes 1179656 | tf_op jit(solution)/shard_map/ppermute | solution.py:35
  15.4 3.2 %collective-permute-done.7 = bf16[3,96,192]{2,1,0:T(8,128)(2,1)S(1)} collective-permute-done((bf16[3,96,192]{2,1,0:T(8,128)(2,1)S(1)}, bf16[3,96,192]{2,1,0:T(8,128)(2,1)S(1)}, u32[]{:S(2)}, u32[]{:S(2)}) %collective-permute-start.7) | collective-permute-done | bytes 110624 | tf_op jit(solution)/shard_map/ppermute | solution.py:35
  18.6 2.3 collective-permute-done.6
  26.3 8.1 %collective-permute-done.4.refs_3_ = bf16[256,768]{1,0:T(8,128)(2,1)} collective-permute-done((bf16[256,768]{1,0:T(8,128)(2,1)}, bf16[256,768]{1,0:T(8,128)(2,1)}, u32[]{:S(2)}, u32[]{:S(2)}) %collective-permute-start.4) | collective-permute-done | bytes 393248 | tf_op jit(solution)/shard_map/ppermute | solution.py:35
  35.2 5.4 %qkv.1 = (bf16[4,256,256]{2,1,0:T(8,128)(2,1)}, bf16[2,4,256,256]{3,2,1,0:T(8,128)(2,1)}) custom-call(s32[3,8]{1,0:T(4,128)} %pad_add_fusion.places, bf16[256,768]{1,0:T(8,128)(2,1)} %bitcast.28.refs_0_.refs_12_, bf16[256,768]{1,0:T(8,128)(2,1)} %copy-done.58, bf16[256,768]{1,0:T(8,128)(2,1)} %collective-permute-done.3.refs_2_, ...), custom_call_target="tpu_custom_call" | custom-call | flops 5500000256 | bytes 5000000 | tf_op jit(solution)/shard_map/qkv/pallas_call | solution.py:259
  40.6 3.2 %turn_tokens.1.refs_0_ = bf16[768,1024]{1,0:T(8,128)(2,1)} custom-call(bf16[256,768]{1,0:T(8,128)(2,1)} %bitcast.28.refs_0_.refs_12_, bf16[256,768]{1,0:T(8,128)(2,1)} %copy-done.58, bf16[256,768]{1,0:T(8,128)(2,1)} %collective-permute-done.3.refs_2_, bf16[256,768]{1,0:T(8,128)(2,1)} %collective-permute-done.4.refs_3_), custom_call_target="tpu_custom_call" | custom-call | flops 2200000000 | bytes 2000000 | tf_op jit(solution)/shard_map/turn_tokens/pallas_call | solution.py:279
  43.8 5.8 %collective-permute-done.1.refs_1_ = bf16[480,768]{1,0:T(8,128)(2,1)} collective-permute-done((bf16[480,768]{1,0:T(8,128)(2,1)S(1)}, bf16[480,768]{1,0:T(8,128)(2,1)}, u32[]{:S(2)}, u32[]{:S(2)}) %collective-permute-start.1) | collective-permute-done | bytes 737312 | tf_op jit(solution)/shard_map/ppermute | solution.py:35
  55.3 11.5 %attend.1 = (f32[4,256,256]{2,1,0:T(8,128)}, f32[4,256,256]{2,1,0:T(8,128)}, bf16[256,256]{1,0:T(8,128)(2,1)}, bf16[256,256]{1,0:T(8,128)(2,1)}, bf16[256,256]{1,0:T(8,128)(2,1)}, /*index=5*/bf16[256,256]{1,0:T(8,128)(2,1)}) custom-call(bf16[4,256,256]{2,1,0:T(8,128)(2,1)} %get-tuple-element.266.refs_0_, ...), custom_call_target="tpu_custom_call" | custom-call | flops 13200000000 | bytes 12000000 | tf_op jit(solution)/shard_map/attend/pallas_call | solution.py:417
  66.8 3.1 %collective-permute-done.12.refs_2_ = bf16[496,768]{1,0:T(8,128)(2,1)S(1)} collective-permute-done((bf16[496,768]{1,0:T(8,128)(2,1)S(1)}, bf16[496,768]{1,0:T(8,128)(2,1)S(1)}, u32[]{:S(2)}, u32[]{:S(2)}) %collective-permute-start.12) | collective-permute-done | bytes 761888 | tf_op jit(solution)/shard_map/ppermute | solution.py:35
  75.0 2.5 collective-permute-done.16.refs_9_
  77.6 3.7 %collective-permute-done.17.refs_10_ = bf16[256,256]{1,0:T(8,128)(2,1)S(1)} collective-permute-done((bf16[256,256]{1,0:T(8,128)(2,1)}, bf16[256,256]{1,0:T(8,128)(2,1)S(1)}, u32[]{:S(2)}, u32[]{:S(2)}) %collective-permute-start.17) | collective-permute-done | bytes 131104 | tf_op jit(solution)/shard_map/ppermute | solution.py:35
  84.1 14.5 %forward_up.1 = (f32[16,768]{1,0:T(8,128)}, f32[256,768]{1,0:T(8,128)}, f32[256,1]{1,0:T(8,128)}, bf16[256,3072]{1,0:T(8,128)(2,1)}, bf16[256,3072]{1,0:T(8,128)...) custom-call(s32[3,8]{1,0:T(4,128)} %pad_add_fusion.places, bf16[496,768]{1,0:T(8,128)(2,1)} %copy-done.7, ...), custom_call_target="tpu_custom_call" | custom-call | flops 12099999744 | bytes 11000000 | tf_op jit(solution)/shard_map/forward_up/pallas_call | solution.py:729
  102.2 9.1 %head.1 = (bf16[256,768]{1,0:T(8,128)(2,1)}, f32[8,768]{1,0:T(8,128)}, f32[8,2432]{1,0:T(8,128)}, f32[256,768]{1,0:T(8,128)}, bf16[256,768]{1,0:T(8,128)(2,1)}) custom-call(s32[3,8]{1,0:T(4,128)} %pad_add_fusion.places, bf16[480,768]{1,0:T(8,128)(2,1)} %copy-done.12, bf16[480,768]{1,0:T(8,128)(2,1)} %collective-permute-done.1.refs_1_, ...), custom_call_target="tpu_custom_call" | custom-call | flops 7699999744 | bytes 7000000 | tf_op jit(solution)/shard_map/head/pallas_call | solution.py:824
  115.1 4.8 %down_gradient.1 = (bf16[2,192,768]{2,1,0:T(8,128)(2,1)}, bf16[2,192,768]{2,1,0:T(8,128)(2,1)}, bf16[192,768]{1,0:T(8,128)(2,1)}, bf16[192,768]{1,0:T(8,128)(2,1)}, f32[384,768]{1,0:T(8,128)}) custom-call(bf16[2304,256]{1,0:T(8,128)(2,1)} %get-tuple-element.210.refs_0_, bf16[2304,256]{1,0:T(8,128)(2,1)} %copy-done.43, ...), custom_call_target="tpu_custom_call" | custom-call | flops 3300000000 | bytes 3000000 | tf_op jit(solution)/shard_map/down_gradient/pallas_call | solution.py:956
  122.3 7.1 %backward_down.1 = (f32[8,768]{1,0:T(8,128)}, bf16[4,256,768]{2,1,0:T(8,128)(2,1)}) custom-call(s32[3,8]{1,0:T(4,128)} %pad_add_fusion.places, bf16[480,768]{1,0:T(8,128)(2,1)} %copy-done.12, bf16[480,768]{1,0:T(8,128)(2,1)} %collective-permute-done.1.refs_1_, bf16[480,768]{1,0:T(8,128)(2,1)} %collective-permute-done.10.refs_2_, ...), custom_call_target="tpu_custom_call" | custom-call | flops 5500000256 | bytes 5000000 | tf_op jit(solution)/shard_map/backward_down/pallas_call | solution.py:860
  129.6 7.9 %backward_up.1 = (f32[8,768]{1,0:T(8,128)}, f32[256,768]{1,0:T(8,128)}, bf16[256,768]{1,0:T(8,128)(2,1)}, bf16[256,256]{1,0:T(8,128)(2,1)}, bf16[256,256]{1,0:T(...) custom-call(s32[3,8]{1,0:T(4,128)} %pad_add_fusion.places, bf16[496,768]{1,0:T(8,128)(2,1)} %copy-done.7, ...), custom_call_target="tpu_custom_call" | custom-call | flops 7699999744 | bytes 7000000 | tf_op jit(solution)/shard_map/backward_up/pallas_call | solution.py:916
  145.1 5.8 %up_gradient.1 = (bf16[2,240,768]{2,1,0:T(8,128)(2,1)}, bf16[2,240,768]{2,1,0:T(8,128)(2,1)}, bf16[240,768]{1,0:T(8,128)(2,1)}, bf16[240,768]{1,0:T(8,128)(2,1)}, f32[480,768]{1,0:T(8,128)}) custom-call(bf16[2304,256]{1,0:T(8,128)(2,1)} %get-tuple-element.210.refs_0_, bf16[2304,256]{1,0:T(8,128)(2,1)} %copy-done.43, ...), custom_call_target="tpu_custom_call" | custom-call | flops 4400000000 | bytes 4000000 | tf_op jit(solution)/shard_map/up_gradient/pallas_call | solution.py:956
  150.9 3.4 %collective-permute-done.36 = bf16[192,768]{1,0:T(8,128)(2,1)S(1)} collective-permute-done((bf16[192,768]{1,0:T(8,128)(2,1)S(1)}, bf16[192,768]{1,0:T(8,128)(2,1)S(1)}, u32[]{:S(2)}, u32[]{:S(2)}) %collective-permute-start.36) | collective-permute-done | bytes 294944 | tf_op jit(solution)/shard_map/ppermute | solution.py:35
  158.5 15.3 %attend_back.2 = (bf16[4,256,128]{2,1,0:T(8,128)(2,1)}, bf16[2,4,256,128]{3,2,1,0:T(8,128)(2,1)}, bf16[2,4,256,128]{3,2,1,0:T(8,128)(2,1)}) custom-call(bf16[4,256,256]{2,1,0:T(8,128)(2,1)} %get-tuple-element.266.refs_0_, f32[4,256,256]{2,1,0:T(8,128)} %get-tuple-element.208.refs_1_, f32[4,256,256]{2,1,0:T(8,128)} %get-tuple-element.209.refs_2_, ...), custom_call_target="tpu_custom_call" | custom-call | flops 16499999744 | bytes 15000000 | tf_op jit(solution)/shard_map/attend_back/pallas_call | solution.py:504
  179.6 2.7 %collective-permute-start.45 = (bf16[192,768]{1,0:T(8,128)(2,1)S(1)}, bf16[192,768]{1,0:T(8,128)(2,1)S(1)}, u32[]{:S(2)}, u32[]{:S(2)}) collective-permute-start(bf16[192,768]{1,0:T(8,128)(2,1)S(1)} %add_convert_fusion.3), channel_id=1, source_target_pairs={{0,24},{1,25},{2,26},{3,27},{4,28},{5,29},{6,30},{7,31},{8,16},{9,... | collective-permute-start | bytes 884744 | tf_op jit(solution)/shard_map/ppermute | solution.py:35
  182.3 9.5 %attend_back.3 = (bf16[4,256,128]{2,1,0:T(8,128)(2,1)}, bf16[2,4,256,128]{3,2,1,0:T(8,128)(2,1)}, bf16[2,4,256,128]{3,2,1,0:T(8,128)(2,1)}) custom-call(bf16[4,256,256]{2,1,0:T(8,128)(2,1)} %get-tuple-element.266.refs_0_, f32[4,256,256]{2,1,0:T(8,128)} %get-tuple-element.208.refs_1_, f32[4,256,256]{2,1,0:T(8,128)} %get-tuple-element.209.refs_2_, ...), custom_call_target="tpu_custom_call" | custom-call | flops 8800000000 | bytes 8000000 | tf_op jit(solution)/shard_map/attend_back/pallas_call | solution.py:504
  193.7 2.6 collective-permute-start.49
  196.3 6.3 %input_weights.1 = (bf16[1168,256]{1,0:T(8,128)(2,1)}, bf16[1168,256]{1,0:T(8,128)(2,1)}) custom-call(s32[3,8]{1,0:T(4,128)} %pad_add_fusion.places, bf16[768,1024]{1,0:T(8,128)(2,1)} %turn_tokens.1.refs_0_, bf16[768,1024]{1,0:T(8,128)(2,1)} %collective-permute-done.26.refs_1_, bf16[4,256,128]{2,1,0:T(8,128)(2,1)} %get-tuple-element.249.refs_2_, ...), custom_call_target="tpu_custom_call" | custom-call | flops 5500000256 | bytes 5000000 | tf_op jit(solution)/shard_map/input_weights/pallas_call | solution.py:1104
  202.6 2.7 %collective-permute-done.49 = bf16[240,768]{1,0:T(8,128)(2,1)} collective-permute-done((bf16[240,768]{1,0:T(8,128)(2,1)S(1)}, bf16[240,768]{1,0:T(8,128)(2,1)}, u32[]{:S(2)}, u32[]{:S(2)}) %collective-permute-start.49) | collective-permute-done | bytes 368672 | tf_op jit(solution)/shard_map/ppermute | solution.py:35
  207.9 2.7 %collective-permute-start.56 = (bf16[240,768]{1,0:T(8,128)(2,1)S(1)}, bf16[240,768]{1,0:T(8,128)(2,1)S(1)}, u32[]{:S(2)}, u32[]{:S(2)}) collective-permute-start(bf16[240,768]{1,0:T(8,128)(2,1)S(1)} %add_convert_fusion.1), channel_id=1, source_target_pairs={{0,24},{1,25},{2,26},{3,27},{4,28},{5,29},{6,30},{7,31},{8,16},{9,... | collective-permute-start | bytes 1105928 | tf_op jit(solution)/shard_map/ppermute | solution.py:35
  217.7 5.8 %input_gradients.1 = (f32[256,768]{1,0:T(8,128)}, bf16[256,768]{1,0:T(8,128)(2,1)}, bf16[256,768]{1,0:T(8,128)(2,1)}, bf16[256,768]{1,0:T(8,128)(2,1)}) custom-call(s32[3,8]{1,0:T(4,128)} %pad_add_fusion.places, bf16[4,3,96,256]{3,2,1,0:T(8,128)(2,1)} %copy-done.10, bf16[4,3,96,256]{3,2,1,0:T(8,128)(2,1)} %copy-done.55, ...), custom_call_target="tpu_custom_call" | custom-call | flops 5500000256 | bytes 5000000 | tf_op jit(solution)/shard_map/input_gradients/pallas_call | solution.py:1161
  228.5 4.9 %collective-permute-done.61 = f32[16,1376]{1,0:T(8,128)S(1)} collective-permute-done((f32[16,1376]{1,0:T(8,128)S(1)}, f32[16,1376]{1,0:T(8,128)S(1)}, u32[]{:S(2)}, u32[]{:S(2)}) %collective-permute-start.61) | collective-permute-done | bytes 88096 | tf_op jit(solution)/shard_map/ppermute | solution.py:35
  235.2 2.3 collective-permute-start.62
  237.5 2.7 %collective-permute-start.57 = (bf16[160,768]{1,0:T(8,128)(2,1)S(1)}, bf16[160,768]{1,0:T(8,128)(2,1)S(1)}, u32[]{:S(2)}, u32[]{:S(2)}) collective-permute-start(bf16[160,768]{1,0:T(8,128)(2,1)S(1)} %add_convert_fusion.5), channel_id=1, source_target_pairs={{0,24},{1,25},{2,26},{3,27},{4,28},{5,29},{6,30},{7,31},{8,16},{9,... | collective-permute-start | bytes 737288 | tf_op jit(solution)/shard_map/ppermute | solution.py:35
  240.4 3.5 %collective-permute-done.59 = bf16[256,768]{1,0:T(8,128)(2,1)S(1)} collective-permute-done((bf16[256,768]{1,0:T(8,128)(2,1)}, bf16[256,768]{1,0:T(8,128)(2,1)S(1)}, u32[]{:S(2)}, u32[]{:S(2)}) %collective-permute-start.59) | collective-permute-done | bytes 393248 | tf_op jit(solution)/shard_map/ppermute | solution.py:35
  243.9 3.6 %collective-permute-done.62 = bf16[192,768]{1,0:T(8,128)(2,1)S(1)} collective-permute-done((bf16[192,768]{1,0:T(8,128)(2,1)S(1)}, bf16[192,768]{1,0:T(8,128)(2,1)S(1)}, u32[]{:S(2)}, u32[]{:S(2)}) %collective-permute-start.62) | collective-permute-done | bytes 294944 | tf_op jit(solution)/shard_map/ppermute | solution.py:35
  247.5 5.7 %collective-permute-done.57 = bf16[160,768]{1,0:T(8,128)(2,1)S(1)} collective-permute-done((bf16[160,768]{1,0:T(8,128)(2,1)S(1)}, bf16[160,768]{1,0:T(8,128)(2,1)S(1)}, u32[]{:S(2)}, u32[]{:S(2)}) %collective-permute-start.57) | collective-permute-done | bytes 245792 | tf_op jit(solution)/shard_map/ppermute | solution.py:35
  (355 shorter events, 88.0 us)
Async XLA Ops:
  0.7 20.3 %collective-permute-start.2 = (bf16[256,768]{1,0:T(8,128)(2,1)}, bf16[256,768]{1,0:T(8,128)(2,1)S(1)}, u32[]{:S(2)}, u32[]{:S(2)}) collective-permute-start(bf16[256,768]{1,0:T(8,128)(2,1)} %bitcast.28.refs_0_.refs_12_), channel_id=1, source_target_pairs={{0,2},{1,3},{2,0},{3,1},{4,6},{5,7},{6,4},{7,5},{8,10},{9,11},{10,... | collective-permute-start | bytes 1179656 | tf_op jit(solution)/shard_map/ppermute | solution.py:35
  3.7 17.3 %collective-permute-start.3 = (bf16[256,768]{1,0:T(8,128)(2,1)}, bf16[256,768]{1,0:T(8,128)(2,1)}, u32[]{:S(2)}, u32[]{:S(2)}) collective-permute-start(bf16[256,768]{1,0:T(8,128)(2,1)} %bitcast.28.refs_0_.refs_12_), channel_id=1, source_target_pairs={{0,4},{1,5},{2,6},{3,7},{4,0},{5,1},{6,2},{7,3},{8,12},{9,13},{10,... | collective-permute-start | bytes 1179656 | tf_op jit(solution)/shard_map/ppermute | solution.py:35
  6.7 14.1 %collective-permute-start.6 = (bf16[3,96,192]{2,1,0:T(8,128)(2,1)S(1)}, bf16[3,96,192]{2,1,0:T(8,128)(2,1)S(1)}, u32[]{:S(2)}, u32[]{:S(2)}) collective-permute-start(bf16[3,96,192]{2,1,0:T(8,128)(2,1)S(1)} %get-tuple-element.385), channel_id=1, source_target_pairs={{0,4},{1,5},{2,6},{3,7},{4,0},{5,1},{6,2},{7,3},{8,12},{9,13},{10,... | collective-permute-start | bytes 331784 | tf_op jit(solution)/shard_map/ppermute | solution.py:35
  24.1 26.1 %collective-permute-start = (bf16[496,768]{1,0:T(8,128)(2,1)S(1)}, bf16[496,768]{1,0:T(8,128)(2,1)S(1)}, u32[]{:S(2)}, u32[]{:S(2)}) collective-permute-start(bf16[496,768]{1,0:T(8,128)(2,1)S(1)} %pad_maximum_fusion.refs_0_), channel_id=1, source_target_pairs={{0,2},{1,3},{2,0},{3,1},{4,6},{5,7},{6,4},{7,5},{8,12},{9,13},{10,... | collective-permute-start | bytes 2285576 | tf_op jit(solution)/shard_map/ppermute | solution.py:35
  25.7 23.9 %collective-permute-start.1 = (bf16[480,768]{1,0:T(8,128)(2,1)S(1)}, bf16[480,768]{1,0:T(8,128)(2,1)}, u32[]{:S(2)}, u32[]{:S(2)}) collective-permute-start(bf16[480,768]{1,0:T(8,128)(2,1)S(1)} %constant_dynamic-update-slice_fusion.refs_0_), channel_id=1, source_target_pairs={{0,4},{1,5},{2,6},{3,7},{4,0},{5,1},{6,2},{7,3},{8,10},{9,11},{10,... | collective-permute-start | bytes 2211848 | tf_op jit(solution)/shard_map/ppermute | solution.py:35
  50.2 16.6 %collective-permute-start.14 = (bf16[496,768]{1,0:T(8,128)(2,1)S(1)}, bf16[496,768]{1,0:T(8,128)(2,1)S(1)}, u32[]{:S(2)}, u32[]{:S(2)}) collective-permute-start(bf16[496,768]{1,0:T(8,128)(2,1)S(1)} %pad_maximum_fusion.refs_0_), channel_id=1, source_target_pairs={{0,1},{1,0},{2,3},{3,2},{4,5},{5,4},{6,7},{7,6},{8,9},{9,8},{10,11... | collective-permute-start | bytes 2285576 | tf_op jit(solution)/shard_map/ppermute | solution.py:35
  50.7 23.1 %collective-permute-start.10 = (bf16[480,768]{1,0:T(8,128)(2,1)}, bf16[480,768]{1,0:T(8,128)(2,1)}, u32[]{:S(2)}, u32[]{:S(2)}) collective-permute-start(bf16[480,768]{1,0:T(8,128)(2,1)} %collective-permute-done.1.refs_1_), channel_id=1, source_target_pairs={{0,2},{1,3},{2,0},{3,1},{4,6},{5,7},{6,4},{7,5},{8,12},{9,13},{10,... | collective-permute-start | bytes 2211848 | tf_op jit(solution)/shard_map/ppermute | solution.py:35
  51.2 18.7 %collective-permute-start.12 = (bf16[496,768]{1,0:T(8,128)(2,1)S(1)}, bf16[496,768]{1,0:T(8,128)(2,1)S(1)}, u32[]{:S(2)}, u32[]{:S(2)}) collective-permute-start(bf16[496,768]{1,0:T(8,128)(2,1)S(1)} %collective-permute-done.refs_1_), channel_id=1, source_target_pairs={{0,4},{1,5},{2,6},{3,7},{4,0},{5,1},{6,2},{7,3},{8,10},{9,11},{10,... | collective-permute-start | bytes 2285576 | tf_op jit(solution)/shard_map/ppermute | solution.py:35
  52.3 18.6 %collective-permute-start.13 = (bf16[496,768]{1,0:T(8,128)(2,1)S(1)}, bf16[496,768]{1,0:T(8,128)(2,1)S(1)}, u32[]{:S(2)}, u32[]{:S(2)}) collective-permute-start(bf16[496,768]{1,0:T(8,128)(2,1)S(1)} %collective-permute-done.refs_1_), channel_id=1, source_target_pairs={{0,8},{1,9},{2,10},{3,11},{4,12},{5,13},{6,14},{7,15},{8,0},{9,1},... | collective-permute-start | bytes 2285576 | tf_op jit(solution)/shard_map/ppermute | solution.py:35
  54.2 16.7 %collective-permute-start.15 = (bf16[496,768]{1,0:T(8,128)(2,1)S(1)}, bf16[496,768]{1,0:T(8,128)(2,1)S(1)}, u32[]{:S(2)}, u32[]{:S(2)}) collective-permute-start(bf16[496,768]{1,0:T(8,128)(2,1)S(1)} %collective-permute-done.refs_1_), channel_id=1, source_target_pairs={{0,1},{1,0},{2,3},{3,2},{4,5},{5,4},{6,7},{7,6},{8,9},{9,8},{10,11... | collective-permute-start | bytes 2285576 | tf_op jit(solution)/shard_map/ppermute | solution.py:35
  81.2 17.4 %collective-permute-start.19 = (bf16[480,768]{1,0:T(8,128)(2,1)S(1)}, bf16[480,768]{1,0:T(8,128)(2,1)}, u32[]{:S(2)}, u32[]{:S(2)}) collective-permute-start(bf16[480,768]{1,0:T(8,128)(2,1)S(1)} %constant_dynamic-update-slice_fusion.refs_0_), channel_id=1, source_target_pairs={{0,2},{1,3},{2,0},{3,1},{4,6},{5,7},{6,4},{7,5},{8,12},{9,13},{10,... | collective-permute-start | bytes 2211848 | tf_op jit(solution)/shard_map/ppermute | solution.py:35
  81.8 16.9 %collective-permute-start.20 = (bf16[480,768]{1,0:T(8,128)(2,1)S(1)}, bf16[480,768]{1,0:T(8,128)(2,1)}, u32[]{:S(2)}, u32[]{:S(2)}) collective-permute-start(bf16[480,768]{1,0:T(8,128)(2,1)S(1)} %constant_dynamic-update-slice_fusion.refs_0_), channel_id=1, source_target_pairs={{0,1},{1,0},{2,3},{3,2},{4,5},{5,4},{6,7},{7,6},{8,9},{9,8},{10,11... | collective-permute-start | bytes 2211848 | tf_op jit(solution)/shard_map/ppermute | solution.py:35
  81.8 16.9 %collective-permute-start.21 = (bf16[480,768]{1,0:T(8,128)(2,1)}, bf16[480,768]{1,0:T(8,128)(2,1)}, u32[]{:S(2)}, u32[]{:S(2)}) collective-permute-start(bf16[480,768]{1,0:T(8,128)(2,1)} %collective-permute-done.1.refs_1_), channel_id=1, source_target_pairs={{0,1},{1,0},{2,3},{3,2},{4,5},{5,4},{6,7},{7,6},{8,9},{9,8},{10,11... | collective-permute-start | bytes 2211848 | tf_op jit(solution)/shard_map/ppermute | solution.py:35
  82.3 16.4 %collective-permute-start.22 = (bf16[480,768]{1,0:T(8,128)(2,1)}, bf16[480,768]{1,0:T(8,128)(2,1)}, u32[]{:S(2)}, u32[]{:S(2)}) collective-permute-start(bf16[480,768]{1,0:T(8,128)(2,1)} %collective-permute-done.10.refs_2_), channel_id=1, source_target_pairs={{0,1},{1,0},{2,3},{3,2},{4,5},{5,4},{6,7},{7,6},{8,9},{9,8},{10,11... | collective-permute-start | bytes 2211848 | tf_op jit(solution)/shard_map/ppermute | solution.py:35
  98.7 23.6 %collective-permute-start.26 = (bf16[768,1024]{1,0:T(8,128)(2,1)S(1)}, bf16[768,1024]{1,0:T(8,128)(2,1)}, u32[]{:S(2)}, u32[]{:S(2)}) collective-permute-start(bf16[768,1024]{1,0:T(8,128)(2,1)S(1)} %copy-done.41), channel_id=1, source_target_pairs={{0,1},{1,0},{2,3},{3,2},{4,5},{5,4},{6,7},{7,6},{8,9},{9,8},{10,11... | collective-permute-start | bytes 4718600 | tf_op jit(solution)/shard_map/ppermute | solution.py:35
  99.2 14.1 %collective-permute-start.27 = (bf16[2304,256]{1,0:T(8,128)(2,1)}, bf16[2304,256]{1,0:T(8,128)(2,1)S(1)}, u32[]{:S(2)}, u32[]{:S(2)}) collective-permute-start(bf16[2304,256]{1,0:T(8,128)(2,1)} %get-tuple-element.211), channel_id=1, source_target_pairs={{0,1},{1,0},{2,3},{3,2},{4,5},{5,4},{6,7},{7,6},{8,9},{9,8},{10,11... | collective-permute-start | bytes 3538952 | tf_op jit(solution)/shard_map/ppermute | solution.py:35
  119.9 18.4 %collective-permute-start.30 = (bf16[2,192,768]{2,1,0:T(8,128)(2,1)}, bf16[2,192,768]{2,1,0:T(8,128)(2,1)S(1)}, u32[]{:S(2)}, u32[]{:S(2)}) collective-permute-start(bf16[2,192,768]{2,1,0:T(8,128)(2,1)} %get-tuple-element.213), channel_id=1, source_target_pairs={{0,2},{1,3},{2,0},{3,1},{4,6},{5,7},{6,4},{7,5},{8,10},{9,11},{10,... | collective-permute-start | bytes 1769480 | tf_op jit(solution)/shard_map/ppermute | solution.py:35
  121.6 16.8 %collective-permute-start.31 = (bf16[2,192,768]{2,1,0:T(8,128)(2,1)}, bf16[2,192,768]{2,1,0:T(8,128)(2,1)S(1)}, u32[]{:S(2)}, u32[]{:S(2)}) collective-permute-start(bf16[2,192,768]{2,1,0:T(8,128)(2,1)} %get-tuple-element.214), channel_id=1, source_target_pairs={{0,4},{1,5},{2,6},{3,7},{4,0},{5,1},{6,2},{7,3},{8,12},{9,13},{10,... | collective-permute-start | bytes 1769480 | tf_op jit(solution)/shard_map/ppermute | solution.py:35
  129.5 14.4 %collective-permute-start.29 = (bf16[4,256,768]{2,1,0:T(8,128)(2,1)}, bf16[4,256,768]{2,1,0:T(8,128)(2,1)S(1)}, u32[]{:S(2)}, u32[]{:S(2)}) collective-permute-start(bf16[4,256,768]{2,1,0:T(8,128)(2,1)} %get-tuple-element.220.refs_10_.refs_2_), channel_id=1, source_target_pairs={{0,1},{1,0},{2,3},{3,2},{4,5},{5,4},{6,7},{7,6},{8,9},{9,8},{10,11... | collective-permute-start | bytes 4718600 | tf_op jit(solution)/shard_map/ppermute | solution.py:35
  154.3 19.5 %collective-permute-start.38 = (f32[8,3968]{1,0:T(8,128)S(1)}, f32[8,3968]{1,0:T(8,128)S(1)}, u32[]{:S(2)}, u32[]{:S(2)}) collective-permute-start(f32[8,3968]{1,0:T(8,128)S(1)} %pad_maximum_fusion.6), channel_id=1, source_target_pairs={{0,1},{1,0},{2,3},{3,2},{4,5},{5,4},{6,7},{7,6},{8,9},{9,8},{10,11... | collective-permute-start | bytes 380936 | tf_op jit(solution)/shard_map/ppermute | solution.py:35
  154.6 19.2 %collective-permute-start.39 = (bf16[192,768]{1,0:T(8,128)(2,1)S(1)}, bf16[192,768]{1,0:T(8,128)(2,1)S(1)}, u32[]{:S(2)}, u32[]{:S(2)}) collective-permute-start(bf16[192,768]{1,0:T(8,128)(2,1)S(1)} %select_convert_fusion.2), channel_id=1, source_target_pairs={{0,8},{1,9},{2,10},{3,11},{4,12},{5,13},{6,14},{7,15},{8,0},{9,1},... | collective-permute-start | bytes 884744 | tf_op jit(solution)/shard_map/ppermute | solution.py:35
  156.8 18.8 %collective-permute-start.40 = (bf16[2,240,768]{2,1,0:T(8,128)(2,1)}, bf16[2,240,768]{2,1,0:T(8,128)(2,1)S(1)}, u32[]{:S(2)}, u32[]{:S(2)}) collective-permute-start(bf16[2,240,768]{2,1,0:T(8,128)(2,1)} %get-tuple-element.257), channel_id=1, source_target_pairs={{0,2},{1,3},{2,0},{3,1},{4,6},{5,7},{6,4},{7,5},{8,10},{9,11},{10,... | collective-permute-start | bytes 2211848 | tf_op jit(solution)/shard_map/ppermute | solution.py:35
  157.3 18.3 %collective-permute-start.41 = (bf16[2,240,768]{2,1,0:T(8,128)(2,1)S(1)}, bf16[2,240,768]{2,1,0:T(8,128)(2,1)S(1)}, u32[]{:S(2)}, u32[]{:S(2)}) collective-permute-start(bf16[2,240,768]{2,1,0:T(8,128)(2,1)S(1)} %copy-done.54), channel_id=1, source_target_pairs={{0,4},{1,5},{2,6},{3,7},{4,0},{5,1},{6,2},{7,3},{8,12},{9,13},{10,... | collective-permute-start | bytes 2211848 | tf_op jit(solution)/shard_map/ppermute | solution.py:35
  175.7 16.1 %collective-permute-start.42 = (f32[8,3968]{1,0:T(8,128)S(1)}, f32[8,3968]{1,0:T(8,128)S(1)}, u32[]{:S(2)}, u32[]{:S(2)}) collective-permute-start(f32[8,3968]{1,0:T(8,128)S(1)} %add.230), channel_id=1, source_target_pairs={{0,2},{1,3},{2,0},{3,1},{4,6},{5,7},{6,4},{7,5},{8,10},{9,11},{10,... | collective-permute-start | bytes 380936 | tf_op jit(solution)/shard_map/ppermute | solution.py:35
  177.3 14.5 %collective-permute-start.43 = (bf16[240,768]{1,0:T(8,128)(2,1)S(1)}, bf16[240,768]{1,0:T(8,128)(2,1)S(1)}, u32[]{:S(2)}, u32[]{:S(2)}) collective-permute-start(bf16[240,768]{1,0:T(8,128)(2,1)S(1)} %fusion.7), channel_id=1, source_target_pairs={{0,4},{1,5},{2,6},{3,7},{4,0},{5,1},{6,2},{7,3},{8,12},{9,13},{10,... | collective-permute-start | bytes 1105928 | tf_op jit(solution)/shard_map/ppermute | solution.py:35
  178.0 13.9 %collective-permute-start.44 = (bf16[240,768]{1,0:T(8,128)(2,1)S(1)}, bf16[240,768]{1,0:T(8,128)(2,1)S(1)}, u32[]{:S(2)}, u32[]{:S(2)}) collective-permute-start(bf16[240,768]{1,0:T(8,128)(2,1)S(1)} %fusion.6), channel_id=1, source_target_pairs={{0,2},{1,3},{2,0},{3,1},{4,6},{5,7},{6,4},{7,5},{8,10},{9,11},{10,... | collective-permute-start | bytes 1105928 | tf_op jit(solution)/shard_map/ppermute | solution.py:35
  182.3 20.3 %collective-permute-start.46 = (bf16[2,4,256,128]{3,2,1,0:T(8,128)(2,1)}, bf16[2,4,256,128]{3,2,1,0:T(8,128)(2,1)S(1)}, u32[]{:S(2)}, u32[]{:S(2)}) collective-permute-start(bf16[2,4,256,128]{3,2,1,0:T(8,128)(2,1)} %get-tuple-element.269.refs_5_), channel_id=1, source_target_pairs={{0,1},{1,0},{2,3},{3,2},{4,5},{5,4},{6,7},{7,6},{8,9},{9,8},{10,11... | collective-permute-start | bytes 1572872 | tf_op jit(solution)/shard_map/ppermute | solution.py:35
  207.9 27.3 %collective-permute-start.56 = (bf16[240,768]{1,0:T(8,128)(2,1)S(1)}, bf16[240,768]{1,0:T(8,128)(2,1)S(1)}, u32[]{:S(2)}, u32[]{:S(2)}) collective-permute-start(bf16[240,768]{1,0:T(8,128)(2,1)S(1)} %add_convert_fusion.1), channel_id=1, source_target_pairs={{0,24},{1,25},{2,26},{3,27},{4,28},{5,29},{6,30},{7,31},{8,16},{9,... | collective-permute-start | bytes 1105928 | tf_op jit(solution)/shard_map/ppermute | solution.py:35
  224.2 16.1 %collective-permute-start.58 = (bf16[256,768]{1,0:T(8,128)(2,1)}, bf16[256,768]{1,0:T(8,128)(2,1)S(1)}, u32[]{:S(2)}, u32[]{:S(2)}) collective-permute-start(bf16[256,768]{1,0:T(8,128)(2,1)} %get-tuple-element.306), channel_id=1, source_target_pairs={{0,2},{1,3},{2,0},{3,1},{4,6},{5,7},{6,4},{7,5},{8,10},{9,11},{10,... | collective-permute-start | bytes 1179656 | tf_op jit(solution)/shard_map/ppermute | solution.py:35
  225.4 18.5 %collective-permute-start.59 = (bf16[256,768]{1,0:T(8,128)(2,1)}, bf16[256,768]{1,0:T(8,128)(2,1)S(1)}, u32[]{:S(2)}, u32[]{:S(2)}) collective-permute-start(bf16[256,768]{1,0:T(8,128)(2,1)} %get-tuple-element.307), channel_id=1, source_target_pairs={{0,4},{1,5},{2,6},{3,7},{4,0},{5,1},{6,2},{7,3},{8,12},{9,13},{10,... | collective-permute-start | bytes 1179656 | tf_op jit(solution)/shard_map/ppermute | solution.py:35
  237.5 15.7 %collective-permute-start.57 = (bf16[160,768]{1,0:T(8,128)(2,1)S(1)}, bf16[160,768]{1,0:T(8,128)(2,1)S(1)}, u32[]{:S(2)}, u32[]{:S(2)}) collective-permute-start(bf16[160,768]{1,0:T(8,128)(2,1)S(1)} %add_convert_fusion.5), channel_id=1, source_target_pairs={{0,24},{1,25},{2,26},{3,27},{4,28},{5,29},{6,30},{7,31},{8,16},{9,... | collective-permute-start | bytes 737288 | tf_op jit(solution)/shard_map/ppermute | solution.py:35
  240.3 20.9 %collective-permute-start.64 = (bf16[240,768]{1,0:T(8,128)(2,1)S(1)}, bf16[240,768]{1,0:T(8,128)(2,1)S(1)}, u32[]{:S(2)}, u32[]{:S(2)}) collective-permute-start(bf16[240,768]{1,0:T(8,128)(2,1)S(1)} %add_convert_fusion), channel_id=1, source_target_pairs={{0,8},{1,9},{2,10},{3,11},{4,12},{5,13},{6,14},{7,15},{8,0},{9,1},... | collective-permute-start | bytes 1105928 | tf_op jit(solution)/shard_map/ppermute | solution.py:35
  (104 other events, 754.1 us)
where the time goes:
time: 268 us; the launch traced here: 265 us
  Pallas kernels  106 us (40%)
  starting transfers between devices  62 us (23%)
  waiting for transfers between devices  59.8 us (22%)
  other arithmetic  17.5 us (7%)
  local copies, waits for them, and re-layouts  15.1 us (6%)
    ppermute x65, starting transfers between devices, swap(): return lax.ppermute(value, ('dp', 'seq'), pairs)  62 us
    ppermute x65, waiting for transfers between devices, swap(): return lax.ppermute(value, ('dp', 'seq'), pairs)  59.8 us
    pallas_call x2, Pallas kernels, attend_back(): call(functools.partial(attend_back_kernel, len(keyvals), docs, heads), 'a...  24.9 us
    pallas_call x1, Pallas kernels, first_part(): call(functools.partial(first_kernel, count, slots, groups), 'forward_up',...  14.5 us
    pallas_call x1, Pallas kernels, attend(): call(functools.partial(attend_kernel, len(keyvals), docs, slots > 1), 'at...  11.5 us
    pallas_call x2, Pallas kernels, gradient_call(): call(body, name, micros, out_shape=outs, in_specs=[ANY] * len(ins), out_s...  10.6 us
    unnamed x144, local copies, waits for them, and re-layouts  9.12 us
    pallas_call x1, Pallas kernels, head_part(): call(functools.partial(head_kernel, count, docs), 'head', 7, out_shape=ou...  9.11 us
  transfers between devices with their start and end apart: 65, of which 19 were waited for; matrix products, arithmetic and copies ran while one was open for 9% of the time, Pallas kernels for 40%

commit v1 on v0

--- a/solution.py
+++ b/solution.py
@@ -1436,6 +1436,20 @@
         logits = pack[:, 3 * D + CLASSES : 3 * D + 2 * CLASSES]
         return jnp.concatenate(parts, axis=1), logits
 
+    def from_docs(every_doc):
+        pre_all, first_all, pooled_all = (
+            every_doc[:, at : at + size] for at, size in ((0, D), (D, share), (D + share, share))
+        )
+        logit_all = every_doc[:, D + 2 * share : D + 2 * share + CLASSES]
+        lines = jnp.sum(every_doc[:, D + 2 * share + PAIR :].reshape(-1, docs, 3 * share), axis=0)
+        exact = functools.partial(jnp.dot, precision=lax.Precision.HIGHEST)
+        pool_bgrad = lax.dynamic_slice_in_dim(jnp.sum(pre_all, axis=0), me * share, share, 0)
+        return (
+            lines.reshape(3 * docs, share),
+            (exact(first_all.T, pre_all), pool_bgrad),
+            (exact(pooled_all.T, logit_all), jnp.sum(logit_all, axis=0)),
+        )
+
     qkv_parts = input_gradient(places, tokens_t, grad_qs, partial, slots)
     if small_mesh:
         qkv_parts, changes, pack, come, up_dp.come, down_dp.cross = after(
@@ -1470,16 +1484,18 @@
         pack = jnp.concatenate([pack, come], axis=0)
         come = swap(pack, lambda z, i: (z ^ 2, i))
         down_dp.finish()
+        qkv_dp.come, up_dp.cross, sums, input_grad = after(
+            (qkv_dp.come, up_dp.cross, sums, input_grad), qkv_dp.come
+        )
+        qkv_dp.across()
+        sums, input_grad = after((sums, input_grad), qkv_dp.pair)
         sums = exchange([input_grad, *sums])
-        qkv_dp.come, up_dp.cross = after((qkv_dp.come, up_dp.cross), qkv_dp.come)
-        qkv_dp.across()
         up_dp.finish()
-        every_doc = jnp.concatenate([pack, come], axis=0)
-        qkv_dp.cross, sums, every_doc, down_dp.last = after(
-            (qkv_dp.cross, sums, every_doc, down_dp.last), qkv_dp.cross
-        )
+        of_docs = from_docs(jnp.concatenate([pack, come], axis=0))
+        down_wgrad = down_dp.back()
+        qkv_dp.cross, of_docs, down_wgrad = after((qkv_dp.cross, of_docs, down_wgrad), qkv_dp.cross)
         qkv_dp.finish()
-        down_wgrad, up_wgrad = down_dp.back(), up_dp.back()
+        up_wgrad = up_dp.back()
         input_grad = add(*sums)
         qkv_wgrad = qkv_dp.back()
     else:
@@ -1495,18 +1511,8 @@
     qkv_wgrad = qkv_wgrad[: 3 * share].reshape(3, share, D)
     if not small_mesh:
         pack, logits = own_shares(pack)
-        every_doc = stack_dp(pack)
-    pre_all, first_all, pooled_all = (
-        every_doc[:, at : at + size] for at, size in ((0, D), (D, share), (D + share, share))
-    )
-    logit_all = every_doc[:, D + 2 * share : D + 2 * share + CLASSES]
-    lines = jnp.sum(every_doc[:, D + 2 * share + PAIR :].reshape(-1, docs, 3 * share), axis=0)
-    lines = lines.reshape(3 * docs, share)
-
-    def my_share(vector):
-        return lax.dynamic_slice_in_dim(vector, me * share, share, 0)
-
-    exact = functools.partial(jnp.dot, precision=lax.Precision.HIGHEST)
+        of_docs = from_docs(stack_dp(pack))
+    lines, of_pool, of_class = of_docs
     return (
         output[None],
         logits[None],
@@ -1526,10 +1532,8 @@
         lines[0],
         lines[1],
         lines[2],
-        exact(first_all.T, pre_all),
-        my_share(jnp.sum(pre_all, axis=0)),
-        exact(pooled_all.T, logit_all),
-        jnp.sum(logit_all, axis=0),
+        *of_pool,
+        *of_class,
     )
 
 

time: 268 us -> 263 us (0.981)
  waiting for transfers between devices: 59.8 us -> 55.6 us
    ppermute x65, waiting for transfers between devices: 59.8 us -> 55.6 us  [swap(): return lax.ppermute(value, ('dp', 'seq'), pairs)]
    unnamed x144 -> x140, local copies, waits for them, and re-layouts: 9.12 us -> 9.1 us
  transfers between devices with their start and end apart: 65 -> 65, of which waited for: 19 -> 18; matrix products, arithmetic and copies ran while one was open for 9% -> 9% of each run, Pallas kernels for 40% -> 41%
where the time goes in v1:
time: 263 us; the launch traced here: 260 us
  Pallas kernels  106 us (40%)
  starting transfers between devices  62.5 us (24%)
  waiting for transfers between devices  55.6 us (21%)
  other arithmetic  16.4 us (6%)
  local copies, waits for them, and re-layouts  15.1 us (6%)
    ppermute x65, starting transfers between devices, swap(): return lax.ppermute(value, ('dp', 'seq'), pairs)  62.5 us
    ppermute x65, waiting for transfers between devices, swap(): return lax.ppermute(value, ('dp', 'seq'), pairs)  55.6 us
    pallas_call x2, Pallas kernels, attend_back(): call(functools.partial(attend_back_kernel, len(keyvals), docs, heads), 'a...  24.8 us
    pallas_call x1, Pallas kernels, first_part(): call(functools.partial(first_kernel, count, slots, groups), 'forward_up',...  14.5 us
    pallas_call x1, Pallas kernels, attend(): call(functools.partial(attend_kernel, len(keyvals), docs, slots > 1), 'at...  11.5 us
    pallas_call x2, Pallas kernels, gradient_call(): call(body, name, micros, out_shape=outs, in_specs=[ANY] * len(ins), out_s...  10.6 us
    pallas_call x1, Pallas kernels, head_part(): call(functools.partial(head_kernel, count, docs), 'head', 7, out_shape=ou...  9.11 us
    unnamed x140, local copies, waits for them, and re-layouts  9.1 us
  transfers between devices with their start and end apart: 65, of which 18 were waited for; matrix products, arithmetic and copies ran while one was open for 9% of the time, Pallas kernels for 41%

profile of v1, /device:TPU:0, one launch (start us, length us, event | category | flops | bytes accessed | tf_op | source)
XLA Modules:
  0.0 260.3 jit_solution(3040075485496616135)
XLA Ops:
  0.7 3.0 %collective-permute-start.2 = (bf16[256,768]{1,0:T(8,128)(2,1)}, bf16[256,768]{1,0:T(8,128)(2,1)S(1)}, u32[]{:S(2)}, u32[]{:S(2)}) collective-permute-start(bf16[256,768]{1,0:T(8,128)(2,1)} %bitcast.28.refs_0_.refs_12_), channel_id=1, source_target_pairs={{0,2},{1,3},{2,0},{3,1},{4,6},{5,7},{6,4},{7,5},{8,10},{9,11},{10,... | collective-permute-start | bytes 1179656 | tf_op jit(solution)/shard_map/ppermute | solution.py:35
  6.7 2.0 collective-permute-start.6
  15.4 3.2 %collective-permute-done.7 = bf16[3,96,192]{2,1,0:T(8,128)(2,1)S(1)} collective-permute-done((bf16[3,96,192]{2,1,0:T(8,128)(2,1)S(1)}, bf16[3,96,192]{2,1,0:T(8,128)(2,1)S(1)}, u32[]{:S(2)}, u32[]{:S(2)}) %collective-permute-start.7) | collective-permute-done | bytes 110624 | tf_op jit(solution)/shard_map/ppermute | solution.py:35
  18.6 2.3 collective-permute-done.6
  26.3 8.1 %collective-permute-done.4.refs_3_ = bf16[256,768]{1,0:T(8,128)(2,1)} collective-permute-done((bf16[256,768]{1,0:T(8,128)(2,1)}, bf16[256,768]{1,0:T(8,128)(2,1)}, u32[]{:S(2)}, u32[]{:S(2)}) %collective-permute-start.4) | collective-permute-done | bytes 393248 | tf_op jit(solution)/shard_map/ppermute | solution.py:35
  35.2 5.4 %qkv.1 = (bf16[4,256,256]{2,1,0:T(8,128)(2,1)}, bf16[2,4,256,256]{3,2,1,0:T(8,128)(2,1)}) custom-call(s32[3,8]{1,0:T(4,128)} %pad_add_fusion.places, bf16[256,768]{1,0:T(8,128)(2,1)} %bitcast.28.refs_0_.refs_12_, bf16[256,768]{1,0:T(8,128)(2,1)} %copy-done.56, bf16[256,768]{1,0:T(8,128)(2,1)} %collective-permute-done.3.refs_2_, ...), custom_call_target="tpu_custom_call" | custom-call | flops 5500000256 | bytes 5000000 | tf_op jit(solution)/shard_map/qkv/pallas_call | solution.py:259
  40.6 3.2 %turn_tokens.1.refs_0_ = bf16[768,1024]{1,0:T(8,128)(2,1)} custom-call(bf16[256,768]{1,0:T(8,128)(2,1)} %bitcast.28.refs_0_.refs_12_, bf16[256,768]{1,0:T(8,128)(2,1)} %copy-done.56, bf16[256,768]{1,0:T(8,128)(2,1)} %collective-permute-done.3.refs_2_, bf16[256,768]{1,0:T(8,128)(2,1)} %collective-permute-done.4.refs_3_), custom_call_target="tpu_custom_call" | custom-call | flops 2200000000 | bytes 2000000 | tf_op jit(solution)/shard_map/turn_tokens/pallas_call | solution.py:279
  43.8 5.9 %collective-permute-done.1.refs_1_ = bf16[480,768]{1,0:T(8,128)(2,1)} collective-permute-done((bf16[480,768]{1,0:T(8,128)(2,1)S(1)}, bf16[480,768]{1,0:T(8,128)(2,1)}, u32[]{:S(2)}, u32[]{:S(2)}) %collective-permute-start.1) | collective-permute-done | bytes 737312 | tf_op jit(solution)/shard_map/ppermute | solution.py:35
  55.3 11.5 %attend.1 = (f32[4,256,256]{2,1,0:T(8,128)}, f32[4,256,256]{2,1,0:T(8,128)}, bf16[256,256]{1,0:T(8,128)(2,1)}, bf16[256,256]{1,0:T(8,128)(2,1)}, bf16[256,256]{1,0:T(8,128)(2,1)}, /*index=5*/bf16[256,256]{1,0:T(8,128)(2,1)}) custom-call(bf16[4,256,256]{2,1,0:T(8,128)(2,1)} %get-tuple-element.274.refs_0_, ...), custom_call_target="tpu_custom_call" | custom-call | flops 13200000000 | bytes 12000000 | tf_op jit(solution)/shard_map/attend/pallas_call | solution.py:417
  66.8 3.1 %collective-permute-done.12.refs_2_ = bf16[496,768]{1,0:T(8,128)(2,1)S(1)} collective-permute-done((bf16[496,768]{1,0:T(8,128)(2,1)S(1)}, bf16[496,768]{1,0:T(8,128)(2,1)S(1)}, u32[]{:S(2)}, u32[]{:S(2)}) %collective-permute-start.12) | collective-permute-done | bytes 761888 | tf_op jit(solution)/shard_map/ppermute | solution.py:35
  75.0 2.5 collective-permute-done.16.refs_9_
  77.6 3.7 %collective-permute-done.17.refs_10_ = bf16[256,256]{1,0:T(8,128)(2,1)S(1)} collective-permute-done((bf16[256,256]{1,0:T(8,128)(2,1)}, bf16[256,256]{1,0:T(8,128)(2,1)S(1)}, u32[]{:S(2)}, u32[]{:S(2)}) %collective-permute-start.17) | collective-permute-done | bytes 131104 | tf_op jit(solution)/shard_map/ppermute | solution.py:35
  84.1 14.5 %forward_up.1 = (f32[16,768]{1,0:T(8,128)}, f32[256,768]{1,0:T(8,128)}, f32[256,1]{1,0:T(8,128)}, bf16[256,3072]{1,0:T(8,128)(2,1)}, bf16[256,3072]{1,0:T(8,128)...) custom-call(s32[3,8]{1,0:T(4,128)} %pad_add_fusion.places, bf16[496,768]{1,0:T(8,128)(2,1)} %copy-done.7, ...), custom_call_target="tpu_custom_call" | custom-call | flops 12099999744 | bytes 11000000 | tf_op jit(solution)/shard_map/forward_up/pallas_call | solution.py:729
  99.3 2.0 collective-permute-done.25.refs_7_
  102.2 9.1 %head.1 = (bf16[256,768]{1,0:T(8,128)(2,1)}, f32[8,768]{1,0:T(8,128)}, f32[8,2432]{1,0:T(8,128)}, f32[256,768]{1,0:T(8,128)}, bf16[256,768]{1,0:T(8,128)(2,1)}) custom-call(s32[3,8]{1,0:T(4,128)} %pad_add_fusion.places, bf16[480,768]{1,0:T(8,128)(2,1)} %copy-done.12, bf16[480,768]{1,0:T(8,128)(2,1)} %collective-permute-done.1.refs_1_, ...), custom_call_target="tpu_custom_call" | custom-call | flops 7699999744 | bytes 7000000 | tf_op jit(solution)/shard_map/head/pallas_call | solution.py:824
  115.1 4.8 %down_gradient.1 = (bf16[2,192,768]{2,1,0:T(8,128)(2,1)}, bf16[2,192,768]{2,1,0:T(8,128)(2,1)}, bf16[192,768]{1,0:T(8,128)(2,1)}, bf16[192,768]{1,0:T(8,128)(2,1)}, f32[384,768]{1,0:T(8,128)}) custom-call(bf16[2304,256]{1,0:T(8,128)(2,1)} %get-tuple-element.218.refs_0_, bf16[2304,256]{1,0:T(8,128)(2,1)} %copy-done.40, ...), custom_call_target="tpu_custom_call" | custom-call | flops 3300000000 | bytes 3000000 | tf_op jit(solution)/shard_map/down_gradient/pallas_call | solution.py:956
  122.3 7.1 %backward_down.1 = (f32[8,768]{1,0:T(8,128)}, bf16[4,256,768]{2,1,0:T(8,128)(2,1)}) custom-call(s32[3,8]{1,0:T(4,128)} %pad_add_fusion.places, bf16[480,768]{1,0:T(8,128)(2,1)} %copy-done.12, bf16[480,768]{1,0:T(8,128)(2,1)} %collective-permute-done.1.refs_1_, bf16[480,768]{1,0:T(8,128)(2,1)} %collective-permute-done.10.refs_2_, ...), custom_call_target="tpu_custom_call" | custom-call | flops 5500000256 | bytes 5000000 | tf_op jit(solution)/shard_map/backward_down/pallas_call | solution.py:860
  129.6 7.9 %backward_up.1 = (f32[8,768]{1,0:T(8,128)}, f32[256,768]{1,0:T(8,128)}, bf16[256,768]{1,0:T(8,128)(2,1)}, bf16[256,256]{1,0:T(8,128)(2,1)}, bf16[256,256]{1,0:T(...) custom-call(s32[3,8]{1,0:T(4,128)} %pad_add_fusion.places, bf16[496,768]{1,0:T(8,128)(2,1)} %copy-done.7, ...), custom_call_target="tpu_custom_call" | custom-call | flops 7699999744 | bytes 7000000 | tf_op jit(solution)/shard_map/backward_up/pallas_call | solution.py:916
  145.1 5.8 %up_gradient.1 = (bf16[2,240,768]{2,1,0:T(8,128)(2,1)}, bf16[2,240,768]{2,1,0:T(8,128)(2,1)}, bf16[240,768]{1,0:T(8,128)(2,1)}, bf16[240,768]{1,0:T(8,128)(2,1)}, f32[480,768]{1,0:T(8,128)}) custom-call(bf16[2304,256]{1,0:T(8,128)(2,1)} %get-tuple-element.218.refs_0_, bf16[2304,256]{1,0:T(8,128)(2,1)} %copy-done.40, ...), custom_call_target="tpu_custom_call" | custom-call | flops 4400000000 | bytes 4000000 | tf_op jit(solution)/shard_map/up_gradient/pallas_call | solution.py:956
  150.9 3.4 %collective-permute-done.36 = bf16[192,768]{1,0:T(8,128)(2,1)S(1)} collective-permute-done((bf16[192,768]{1,0:T(8,128)(2,1)S(1)}, bf16[192,768]{1,0:T(8,128)(2,1)S(1)}, u32[]{:S(2)}, u32[]{:S(2)}) %collective-permute-start.36) | collective-permute-done | bytes 294944 | tf_op jit(solution)/shard_map/ppermute | solution.py:35
  154.6 2.2 collective-permute-start.39
  158.5 15.3 %attend_back.2 = (bf16[4,256,128]{2,1,0:T(8,128)(2,1)}, bf16[2,4,256,128]{3,2,1,0:T(8,128)(2,1)}, bf16[2,4,256,128]{3,2,1,0:T(8,128)(2,1)}) custom-call(bf16[4,256,256]{2,1,0:T(8,128)(2,1)} %get-tuple-element.274.refs_0_, f32[4,256,256]{2,1,0:T(8,128)} %get-tuple-element.216.refs_1_, f32[4,256,256]{2,1,0:T(8,128)} %get-tuple-element.217.refs_2_, ...), custom_call_target="tpu_custom_call" | custom-call | flops 16499999744 | bytes 15000000 | tf_op jit(solution)/shard_map/attend_back/pallas_call | solution.py:504
  179.5 2.7 %collective-permute-start.45 = (bf16[192,768]{1,0:T(8,128)(2,1)S(1)}, bf16[192,768]{1,0:T(8,128)(2,1)S(1)}, u32[]{:S(2)}, u32[]{:S(2)}) collective-permute-start(bf16[192,768]{1,0:T(8,128)(2,1)S(1)} %add_convert_fusion.3), channel_id=1, source_target_pairs={{0,24},{1,25},{2,26},{3,27},{4,28},{5,29},{6,30},{7,31},{8,16},{9,... | collective-permute-start | bytes 884744 | tf_op jit(solution)/shard_map/ppermute | solution.py:35
  182.2 9.5 %attend_back.3 = (bf16[4,256,128]{2,1,0:T(8,128)(2,1)}, bf16[2,4,256,128]{3,2,1,0:T(8,128)(2,1)}, bf16[2,4,256,128]{3,2,1,0:T(8,128)(2,1)}) custom-call(bf16[4,256,256]{2,1,0:T(8,128)(2,1)} %get-tuple-element.274.refs_0_, f32[4,256,256]{2,1,0:T(8,128)} %get-tuple-element.216.refs_1_, f32[4,256,256]{2,1,0:T(8,128)} %get-tuple-element.217.refs_2_, ...), custom_call_target="tpu_custom_call" | custom-call | flops 8800000000 | bytes 8000000 | tf_op jit(solution)/shard_map/attend_back/pallas_call | solution.py:504
  193.6 2.4 collective-permute-start.49
  195.9 6.3 %input_weights.1 = (bf16[1168,256]{1,0:T(8,128)(2,1)}, bf16[1168,256]{1,0:T(8,128)(2,1)}) custom-call(s32[3,8]{1,0:T(4,128)} %pad_add_fusion.places, bf16[768,1024]{1,0:T(8,128)(2,1)} %turn_tokens.1.refs_0_, bf16[768,1024]{1,0:T(8,128)(2,1)} %collective-permute-done.26.refs_1_, bf16[4,256,128]{2,1,0:T(8,128)(2,1)} %get-tuple-element.257.refs_2_, ...), custom_call_target="tpu_custom_call" | custom-call | flops 5500000256 | bytes 5000000 | tf_op jit(solution)/shard_map/input_weights/pallas_call | solution.py:1104
  202.3 2.7 %collective-permute-done.49 = bf16[240,768]{1,0:T(8,128)(2,1)} collective-permute-done((bf16[240,768]{1,0:T(8,128)(2,1)S(1)}, bf16[240,768]{1,0:T(8,128)(2,1)}, u32[]{:S(2)}, u32[]{:S(2)}) %collective-permute-start.49) | collective-permute-done | bytes 368672 | tf_op jit(solution)/shard_map/ppermute | solution.py:35
  207.5 2.7 %collective-permute-start.56 = (bf16[240,768]{1,0:T(8,128)(2,1)S(1)}, bf16[240,768]{1,0:T(8,128)(2,1)S(1)}, u32[]{:S(2)}, u32[]{:S(2)}) collective-permute-start(bf16[240,768]{1,0:T(8,128)(2,1)S(1)} %add_convert_fusion.1), channel_id=1, source_target_pairs={{0,24},{1,25},{2,26},{3,27},{4,28},{5,29},{6,30},{7,31},{8,16},{9,... | collective-permute-start | bytes 1105928 | tf_op jit(solution)/shard_map/ppermute | solution.py:35
  217.3 5.8 %input_gradients.1 = (f32[256,768]{1,0:T(8,128)}, bf16[256,768]{1,0:T(8,128)(2,1)}, bf16[256,768]{1,0:T(8,128)(2,1)}, bf16[256,768]{1,0:T(8,128)(2,1)}) custom-call(s32[3,8]{1,0:T(4,128)} %pad_add_fusion.places, bf16[4,3,96,256]{3,2,1,0:T(8,128)(2,1)} %copy-done.10, bf16[4,3,96,256]{3,2,1,0:T(8,128)(2,1)} %copy-done.53, ...), custom_call_target="tpu_custom_call" | custom-call | flops 5500000256 | bytes 5000000 | tf_op jit(solution)/shard_map/input_gradients/pallas_call | solution.py:1161
  227.4 6.4 %collective-permute-done.61 = f32[16,1376]{1,0:T(8,128)S(1)} collective-permute-done((f32[16,1376]{1,0:T(8,128)S(1)}, f32[16,1376]{1,0:T(8,128)S(1)}, u32[]{:S(2)}, u32[]{:S(2)}) %collective-permute-start.61) | collective-permute-done | bytes 88096 | tf_op jit(solution)/shard_map/ppermute | solution.py:35
  242.1 2.8 %collective-permute-start.64 = (bf16[240,768]{1,0:T(8,128)(2,1)S(1)}, bf16[240,768]{1,0:T(8,128)(2,1)S(1)}, u32[]{:S(2)}, u32[]{:S(2)}) collective-permute-start(bf16[240,768]{1,0:T(8,128)(2,1)S(1)} %add_convert_fusion), channel_id=1, source_target_pairs={{0,8},{1,9},{2,10},{3,11},{4,12},{5,13},{6,14},{7,15},{8,0},{9,1},... | collective-permute-start | bytes 1105928 | tf_op jit(solution)/shard_map/ppermute | solution.py:35
  249.9 5.3 %collective-permute-done.64 = bf16[240,768]{1,0:T(8,128)(2,1)S(1)} collective-permute-done((bf16[240,768]{1,0:T(8,128)(2,1)S(1)}, bf16[240,768]{1,0:T(8,128)(2,1)S(1)}, u32[]{:S(2)}, u32[]{:S(2)}) %collective-permute-start.64) | collective-permute-done | bytes 368672 | tf_op jit(solution)/shard_map/ppermute | solution.py:35
  (351 shorter events, 85.4 us)
Async XLA Ops:
  0.7 20.3 %collective-permute-start.2 = (bf16[256,768]{1,0:T(8,128)(2,1)}, bf16[256,768]{1,0:T(8,128)(2,1)S(1)}, u32[]{:S(2)}, u32[]{:S(2)}) collective-permute-start(bf16[256,768]{1,0:T(8,128)(2,1)} %bitcast.28.refs_0_.refs_12_), channel_id=1, source_target_pairs={{0,2},{1,3},{2,0},{3,1},{4,6},{5,7},{6,4},{7,5},{8,10},{9,11},{10,... | collective-permute-start | bytes 1179656 | tf_op jit(solution)/shard_map/ppermute | solution.py:35
  3.7 17.3 %collective-permute-start.3 = (bf16[256,768]{1,0:T(8,128)(2,1)}, bf16[256,768]{1,0:T(8,128)(2,1)}, u32[]{:S(2)}, u32[]{:S(2)}) collective-permute-start(bf16[256,768]{1,0:T(8,128)(2,1)} %bitcast.28.refs_0_.refs_12_), channel_id=1, source_target_pairs={{0,4},{1,5},{2,6},{3,7},{4,0},{5,1},{6,2},{7,3},{8,12},{9,13},{10,... | collective-permute-start | bytes 1179656 | tf_op jit(solution)/shard_map/ppermute | solution.py:35
  6.7 14.1 %collective-permute-start.6 = (bf16[3,96,192]{2,1,0:T(8,128)(2,1)S(1)}, bf16[3,96,192]{2,1,0:T(8,128)(2,1)S(1)}, u32[]{:S(2)}, u32[]{:S(2)}) collective-permute-start(bf16[3,96,192]{2,1,0:T(8,128)(2,1)S(1)} %get-tuple-element.401), channel_id=1, source_target_pairs={{0,4},{1,5},{2,6},{3,7},{4,0},{5,1},{6,2},{7,3},{8,12},{9,13},{10,... | collective-permute-start | bytes 331784 | tf_op jit(solution)/shard_map/ppermute | solution.py:35
  24.1 26.1 %collective-permute-start = (bf16[496,768]{1,0:T(8,128)(2,1)S(1)}, bf16[496,768]{1,0:T(8,128)(2,1)S(1)}, u32[]{:S(2)}, u32[]{:S(2)}) collective-permute-start(bf16[496,768]{1,0:T(8,128)(2,1)S(1)} %pad_maximum_fusion.refs_0_), channel_id=1, source_target_pairs={{0,2},{1,3},{2,0},{3,1},{4,6},{5,7},{6,4},{7,5},{8,12},{9,13},{10,... | collective-permute-start | bytes 2285576 | tf_op jit(solution)/shard_map/ppermute | solution.py:35
  25.7 23.9 %collective-permute-start.1 = (bf16[480,768]{1,0:T(8,128)(2,1)S(1)}, bf16[480,768]{1,0:T(8,128)(2,1)}, u32[]{:S(2)}, u32[]{:S(2)}) collective-permute-start(bf16[480,768]{1,0:T(8,128)(2,1)S(1)} %constant_dynamic-update-slice_fusion.refs_0_), channel_id=1, source_target_pairs={{0,4},{1,5},{2,6},{3,7},{4,0},{5,1},{6,2},{7,3},{8,10},{9,11},{10,... | collective-permute-start | bytes 2211848 | tf_op jit(solution)/shard_map/ppermute | solution.py:35
  50.2 16.6 %collective-permute-start.14 = (bf16[496,768]{1,0:T(8,128)(2,1)S(1)}, bf16[496,768]{1,0:T(8,128)(2,1)S(1)}, u32[]{:S(2)}, u32[]{:S(2)}) collective-permute-start(bf16[496,768]{1,0:T(8,128)(2,1)S(1)} %pad_maximum_fusion.refs_0_), channel_id=1, source_target_pairs={{0,1},{1,0},{2,3},{3,2},{4,5},{5,4},{6,7},{7,6},{8,9},{9,8},{10,11... | collective-permute-start | bytes 2285576 | tf_op jit(solution)/shard_map/ppermute | solution.py:35
  50.7 23.1 %collective-permute-start.10 = (bf16[480,768]{1,0:T(8,128)(2,1)}, bf16[480,768]{1,0:T(8,128)(2,1)}, u32[]{:S(2)}, u32[]{:S(2)}) collective-permute-start(bf16[480,768]{1,0:T(8,128)(2,1)} %collective-permute-done.1.refs_1_), channel_id=1, source_target_pairs={{0,2},{1,3},{2,0},{3,1},{4,6},{5,7},{6,4},{7,5},{8,12},{9,13},{10,... | collective-permute-start | bytes 2211848 | tf_op jit(solution)/shard_map/ppermute | solution.py:35
  51.2 18.7 %collective-permute-start.12 = (bf16[496,768]{1,0:T(8,128)(2,1)S(1)}, bf16[496,768]{1,0:T(8,128)(2,1)S(1)}, u32[]{:S(2)}, u32[]{:S(2)}) collective-permute-start(bf16[496,768]{1,0:T(8,128)(2,1)S(1)} %collective-permute-done.refs_1_), channel_id=1, source_target_pairs={{0,4},{1,5},{2,6},{3,7},{4,0},{5,1},{6,2},{7,3},{8,10},{9,11},{10,... | collective-permute-start | bytes 2285576 | tf_op jit(solution)/shard_map/ppermute | solution.py:35
  52.3 18.6 %collective-permute-start.13 = (bf16[496,768]{1,0:T(8,128)(2,1)S(1)}, bf16[496,768]{1,0:T(8,128)(2,1)S(1)}, u32[]{:S(2)}, u32[]{:S(2)}) collective-permute-start(bf16[496,768]{1,0:T(8,128)(2,1)S(1)} %collective-permute-done.refs_1_), channel_id=1, source_target_pairs={{0,8},{1,9},{2,10},{3,11},{4,12},{5,13},{6,14},{7,15},{8,0},{9,1},... | collective-permute-start | bytes 2285576 | tf_op jit(solution)/shard_map/ppermute | solution.py:35
  54.2 16.7 %collective-permute-start.15 = (bf16[496,768]{1,0:T(8,128)(2,1)S(1)}, bf16[496,768]{1,0:T(8,128)(2,1)S(1)}, u32[]{:S(2)}, u32[]{:S(2)}) collective-permute-start(bf16[496,768]{1,0:T(8,128)(2,1)S(1)} %collective-permute-done.refs_1_), channel_id=1, source_target_pairs={{0,1},{1,0},{2,3},{3,2},{4,5},{5,4},{6,7},{7,6},{8,9},{9,8},{10,11... | collective-permute-start | bytes 2285576 | tf_op jit(solution)/shard_map/ppermute | solution.py:35
  81.2 17.3 %collective-permute-start.19 = (bf16[480,768]{1,0:T(8,128)(2,1)S(1)}, bf16[480,768]{1,0:T(8,128)(2,1)}, u32[]{:S(2)}, u32[]{:S(2)}) collective-permute-start(bf16[480,768]{1,0:T(8,128)(2,1)S(1)} %constant_dynamic-update-slice_fusion.refs_0_), channel_id=1, source_target_pairs={{0,2},{1,3},{2,0},{3,1},{4,6},{5,7},{6,4},{7,5},{8,12},{9,13},{10,... | collective-permute-start | bytes 2211848 | tf_op jit(solution)/shard_map/ppermute | solution.py:35
  81.8 16.8 %collective-permute-start.20 = (bf16[480,768]{1,0:T(8,128)(2,1)S(1)}, bf16[480,768]{1,0:T(8,128)(2,1)}, u32[]{:S(2)}, u32[]{:S(2)}) collective-permute-start(bf16[480,768]{1,0:T(8,128)(2,1)S(1)} %constant_dynamic-update-slice_fusion.refs_0_), channel_id=1, source_target_pairs={{0,1},{1,0},{2,3},{3,2},{4,5},{5,4},{6,7},{7,6},{8,9},{9,8},{10,11... | collective-permute-start | bytes 2211848 | tf_op jit(solution)/shard_map/ppermute | solution.py:35
  81.8 16.8 %collective-permute-start.21 = (bf16[480,768]{1,0:T(8,128)(2,1)}, bf16[480,768]{1,0:T(8,128)(2,1)}, u32[]{:S(2)}, u32[]{:S(2)}) collective-permute-start(bf16[480,768]{1,0:T(8,128)(2,1)} %collective-permute-done.1.refs_1_), channel_id=1, source_target_pairs={{0,1},{1,0},{2,3},{3,2},{4,5},{5,4},{6,7},{7,6},{8,9},{9,8},{10,11... | collective-permute-start | bytes 2211848 | tf_op jit(solution)/shard_map/ppermute | solution.py:35
  82.3 16.3 %collective-permute-start.22 = (bf16[480,768]{1,0:T(8,128)(2,1)}, bf16[480,768]{1,0:T(8,128)(2,1)}, u32[]{:S(2)}, u32[]{:S(2)}) collective-permute-start(bf16[480,768]{1,0:T(8,128)(2,1)} %collective-permute-done.10.refs_2_), channel_id=1, source_target_pairs={{0,1},{1,0},{2,3},{3,2},{4,5},{5,4},{6,7},{7,6},{8,9},{9,8},{10,11... | collective-permute-start | bytes 2211848 | tf_op jit(solution)/shard_map/ppermute | solution.py:35
  98.7 23.6 %collective-permute-start.26 = (bf16[768,1024]{1,0:T(8,128)(2,1)S(1)}, bf16[768,1024]{1,0:T(8,128)(2,1)}, u32[]{:S(2)}, u32[]{:S(2)}) collective-permute-start(bf16[768,1024]{1,0:T(8,128)(2,1)S(1)} %copy-done.38), channel_id=1, source_target_pairs={{0,1},{1,0},{2,3},{3,2},{4,5},{5,4},{6,7},{7,6},{8,9},{9,8},{10,11... | collective-permute-start | bytes 4718600 | tf_op jit(solution)/shard_map/ppermute | solution.py:35
  99.2 14.1 %collective-permute-start.27 = (bf16[2304,256]{1,0:T(8,128)(2,1)}, bf16[2304,256]{1,0:T(8,128)(2,1)S(1)}, u32[]{:S(2)}, u32[]{:S(2)}) collective-permute-start(bf16[2304,256]{1,0:T(8,128)(2,1)} %get-tuple-element.219), channel_id=1, source_target_pairs={{0,1},{1,0},{2,3},{3,2},{4,5},{5,4},{6,7},{7,6},{8,9},{9,8},{10,11... | collective-permute-start | bytes 3538952 | tf_op jit(solution)/shard_map/ppermute | solution.py:35
  119.9 18.4 %collective-permute-start.30 = (bf16[2,192,768]{2,1,0:T(8,128)(2,1)}, bf16[2,192,768]{2,1,0:T(8,128)(2,1)S(1)}, u32[]{:S(2)}, u32[]{:S(2)}) collective-permute-start(bf16[2,192,768]{2,1,0:T(8,128)(2,1)} %get-tuple-element.221), channel_id=1, source_target_pairs={{0,2},{1,3},{2,0},{3,1},{4,6},{5,7},{6,4},{7,5},{8,10},{9,11},{10,... | collective-permute-start | bytes 1769480 | tf_op jit(solution)/shard_map/ppermute | solution.py:35
  121.5 16.8 %collective-permute-start.31 = (bf16[2,192,768]{2,1,0:T(8,128)(2,1)}, bf16[2,192,768]{2,1,0:T(8,128)(2,1)S(1)}, u32[]{:S(2)}, u32[]{:S(2)}) collective-permute-start(bf16[2,192,768]{2,1,0:T(8,128)(2,1)} %get-tuple-element.222), channel_id=1, source_target_pairs={{0,4},{1,5},{2,6},{3,7},{4,0},{5,1},{6,2},{7,3},{8,12},{9,13},{10,... | collective-permute-start | bytes 1769480 | tf_op jit(solution)/shard_map/ppermute | solution.py:35
  129.5 14.4 %collective-permute-start.29 = (bf16[4,256,768]{2,1,0:T(8,128)(2,1)}, bf16[4,256,768]{2,1,0:T(8,128)(2,1)S(1)}, u32[]{:S(2)}, u32[]{:S(2)}) collective-permute-start(bf16[4,256,768]{2,1,0:T(8,128)(2,1)} %get-tuple-element.228.refs_10_.refs_2_), channel_id=1, source_target_pairs={{0,1},{1,0},{2,3},{3,2},{4,5},{5,4},{6,7},{7,6},{8,9},{9,8},{10,11... | collective-permute-start | bytes 4718600 | tf_op jit(solution)/shard_map/ppermute | solution.py:35
  154.3 19.5 %collective-permute-start.38 = (f32[8,3968]{1,0:T(8,128)S(1)}, f32[8,3968]{1,0:T(8,128)S(1)}, u32[]{:S(2)}, u32[]{:S(2)}) collective-permute-start(f32[8,3968]{1,0:T(8,128)S(1)} %pad_maximum_fusion.5), channel_id=1, source_target_pairs={{0,1},{1,0},{2,3},{3,2},{4,5},{5,4},{6,7},{7,6},{8,9},{9,8},{10,11... | collective-permute-start | bytes 380936 | tf_op jit(solution)/shard_map/ppermute | solution.py:35
  154.6 19.2 %collective-permute-start.39 = (bf16[192,768]{1,0:T(8,128)(2,1)S(1)}, bf16[192,768]{1,0:T(8,128)(2,1)S(1)}, u32[]{:S(2)}, u32[]{:S(2)}) collective-permute-start(bf16[192,768]{1,0:T(8,128)(2,1)S(1)} %select_convert_fusion.2), channel_id=1, source_target_pairs={{0,8},{1,9},{2,10},{3,11},{4,12},{5,13},{6,14},{7,15},{8,0},{9,1},... | collective-permute-start | bytes 884744 | tf_op jit(solution)/shard_map/ppermute | solution.py:35
  156.8 18.6 %collective-permute-start.40 = (bf16[2,240,768]{2,1,0:T(8,128)(2,1)S(1)}, bf16[2,240,768]{2,1,0:T(8,128)(2,1)S(1)}, u32[]{:S(2)}, u32[]{:S(2)}) collective-permute-start(bf16[2,240,768]{2,1,0:T(8,128)(2,1)S(1)} %copy-done.52), channel_id=1, source_target_pairs={{0,2},{1,3},{2,0},{3,1},{4,6},{5,7},{6,4},{7,5},{8,10},{9,11},{10,... | collective-permute-start | bytes 2211848 | tf_op jit(solution)/shard_map/ppermute | solution.py:35
  157.3 18.3 %collective-permute-start.41 = (bf16[2,240,768]{2,1,0:T(8,128)(2,1)S(1)}, bf16[2,240,768]{2,1,0:T(8,128)(2,1)S(1)}, u32[]{:S(2)}, u32[]{:S(2)}) collective-permute-start(bf16[2,240,768]{2,1,0:T(8,128)(2,1)S(1)} %copy-done.51), channel_id=1, source_target_pairs={{0,4},{1,5},{2,6},{3,7},{4,0},{5,1},{6,2},{7,3},{8,12},{9,13},{10,... | collective-permute-start | bytes 2211848 | tf_op jit(solution)/shard_map/ppermute | solution.py:35
  175.7 16.1 %collective-permute-start.42 = (f32[8,3968]{1,0:T(8,128)S(1)}, f32[8,3968]{1,0:T(8,128)S(1)}, u32[]{:S(2)}, u32[]{:S(2)}) collective-permute-start(f32[8,3968]{1,0:T(8,128)S(1)} %add.230), channel_id=1, source_target_pairs={{0,2},{1,3},{2,0},{3,1},{4,6},{5,7},{6,4},{7,5},{8,10},{9,11},{10,... | collective-permute-start | bytes 380936 | tf_op jit(solution)/shard_map/ppermute | solution.py:35
  177.3 14.5 %collective-permute-start.43 = (bf16[240,768]{1,0:T(8,128)(2,1)S(1)}, bf16[240,768]{1,0:T(8,128)(2,1)S(1)}, u32[]{:S(2)}, u32[]{:S(2)}) collective-permute-start(bf16[240,768]{1,0:T(8,128)(2,1)S(1)} %fusion.7), channel_id=1, source_target_pairs={{0,4},{1,5},{2,6},{3,7},{4,0},{5,1},{6,2},{7,3},{8,12},{9,13},{10,... | collective-permute-start | bytes 1105928 | tf_op jit(solution)/shard_map/ppermute | solution.py:35
  178.0 13.8 %collective-permute-start.44 = (bf16[240,768]{1,0:T(8,128)(2,1)S(1)}, bf16[240,768]{1,0:T(8,128)(2,1)S(1)}, u32[]{:S(2)}, u32[]{:S(2)}) collective-permute-start(bf16[240,768]{1,0:T(8,128)(2,1)S(1)} %fusion.6), channel_id=1, source_target_pairs={{0,2},{1,3},{2,0},{3,1},{4,6},{5,7},{6,4},{7,5},{8,10},{9,11},{10,... | collective-permute-start | bytes 1105928 | tf_op jit(solution)/shard_map/ppermute | solution.py:35
  182.2 20.0 %collective-permute-start.46 = (bf16[2,4,256,128]{3,2,1,0:T(8,128)(2,1)}, bf16[2,4,256,128]{3,2,1,0:T(8,128)(2,1)S(1)}, u32[]{:S(2)}, u32[]{:S(2)}) collective-permute-start(bf16[2,4,256,128]{3,2,1,0:T(8,128)(2,1)} %get-tuple-element.277.refs_5_), channel_id=1, source_target_pairs={{0,1},{1,0},{2,3},{3,2},{4,5},{5,4},{6,7},{7,6},{8,9},{9,8},{10,11... | collective-permute-start | bytes 1572872 | tf_op jit(solution)/shard_map/ppermute | solution.py:35
  207.5 29.6 %collective-permute-start.56 = (bf16[240,768]{1,0:T(8,128)(2,1)S(1)}, bf16[240,768]{1,0:T(8,128)(2,1)S(1)}, u32[]{:S(2)}, u32[]{:S(2)}) collective-permute-start(bf16[240,768]{1,0:T(8,128)(2,1)S(1)} %add_convert_fusion.1), channel_id=1, source_target_pairs={{0,24},{1,25},{2,26},{3,27},{4,28},{5,29},{6,30},{7,31},{8,16},{9,... | collective-permute-start | bytes 1105928 | tf_op jit(solution)/shard_map/ppermute | solution.py:35
  226.5 15.6 %collective-permute-start.62 = (bf16[192,768]{1,0:T(8,128)(2,1)S(1)}, bf16[192,768]{1,0:T(8,128)(2,1)S(1)}, u32[]{:S(2)}, u32[]{:S(2)}) collective-permute-start(bf16[192,768]{1,0:T(8,128)(2,1)S(1)} %add_convert_fusion.2), channel_id=1, source_target_pairs={{0,8},{1,9},{2,10},{3,11},{4,12},{5,13},{6,14},{7,15},{8,0},{9,1},... | collective-permute-start | bytes 884744 | tf_op jit(solution)/shard_map/ppermute | solution.py:35
  238.5 18.7 %collective-permute-start.59 = (bf16[256,768]{1,0:T(8,128)(2,1)}, bf16[256,768]{1,0:T(8,128)(2,1)S(1)}, u32[]{:S(2)}, u32[]{:S(2)}) collective-permute-start(bf16[256,768]{1,0:T(8,128)(2,1)} %get-tuple-element.324), channel_id=1, source_target_pairs={{0,6},{1,7},{2,4},{3,5},{4,2},{5,3},{6,0},{7,1},{8,14},{9,15},{10,... | collective-permute-start | bytes 1179656 | tf_op jit(solution)/shard_map/ppermute | solution.py:35
  239.9 17.4 %collective-permute-start.58 = (bf16[256,768]{1,0:T(8,128)(2,1)}, bf16[256,768]{1,0:T(8,128)(2,1)S(1)}, u32[]{:S(2)}, u32[]{:S(2)}) collective-permute-start(bf16[256,768]{1,0:T(8,128)(2,1)} %get-tuple-element.323), channel_id=1, source_target_pairs={{0,4},{1,5},{2,6},{3,7},{4,0},{5,1},{6,2},{7,3},{8,12},{9,13},{10,... | collective-permute-start | bytes 1179656 | tf_op jit(solution)/shard_map/ppermute | solution.py:35
  241.4 15.8 %collective-permute-start.57 = (bf16[256,768]{1,0:T(8,128)(2,1)}, bf16[256,768]{1,0:T(8,128)(2,1)S(1)}, u32[]{:S(2)}, u32[]{:S(2)}) collective-permute-start(bf16[256,768]{1,0:T(8,128)(2,1)} %get-tuple-element.322), channel_id=1, source_target_pairs={{0,2},{1,3},{2,0},{3,1},{4,6},{5,7},{6,4},{7,5},{8,10},{9,11},{10,... | collective-permute-start | bytes 1179656 | tf_op jit(solution)/shard_map/ppermute | solution.py:35
  (101 other events, 745.0 us)

commit v2 on v1

--- a/solution.py
+++ b/solution.py
@@ -432,7 +432,16 @@
     return made[0], made[1], list(made[2:])
 
 
-def attend_back_kernel(sides, docs, heads, *refs):
+def head_lanes(ref, first, heads):
+    if first is None:
+        return ref[...]
+    found = ref[:, first : first + heads * HEAD_DIM]
+    if heads > 1:
+        return found
+    return jnp.concatenate([found, jnp.zeros_like(found)], axis=1)
+
+
+def attend_back_kernel(sides, docs, heads, first, *refs):
     query, wide, total, feature_q, feature_k = refs[:5]
     slots, length = feature_q.shape[0], feature_k.shape[0] * ROWS
     grads_in, keyvals = refs[5 : 5 + slots], refs[5 + slots : 5 + slots + sides]
@@ -447,7 +456,7 @@
     units = [(slot, head) for head in range(heads) for slot in range(slots)]
     for unit, (slot, head) in enumerate(units):
         mine, at = sides_of[head], head * HEAD_DIM
-        rows, grads = query[slot] * 0.125, grads_in[slot][...]
+        rows, grads = query[slot] * 0.125, head_lanes(grads_in[slot], first, heads)
         product = jnp.where(mine, grads.astype(F32) * wide[slot], 0.0)
         delta = jnp.sum(product, axis=1, keepdims=True)
         sums = total[slot, :, at : at + 1]
@@ -501,15 +510,19 @@
         jax.ShapeDtypeStruct(a.shape[:-1] + (tiles * PAIR,), BF16) for a in (query, *keyvals)
     )
     units = slots * heads
+    whole = tiles > 1
     made = call(
-        functools.partial(attend_back_kernel, len(keyvals), docs, heads),
+        functools.partial(
+            attend_back_kernel, len(keyvals), docs, heads, None if whole else base * PAIR
+        ),
         "attend_back",
         8 if single else 15,
         grid=(tiles,),
         out_shape=outs,
         in_specs=[tile_spec(a, base) for a in (query, wide, total)]
         + [fixed_spec(feature_q), fixed_spec(feature_k)]
-        + [tile_spec(a, base) for a in (*grads, *keyvals)],
+        + [tile_spec(a, base) if whole else fixed_spec(a) for a in grads]
+        + [tile_spec(a, base) for a in keyvals],
         out_specs=tuple(tile_spec(a) for a in outs),
         scratch_shapes=[
             pltpu.VMEM((heads, length, PAIR), BF16),
@@ -903,9 +916,7 @@
     for s in range(slots):
         first = pl.multiple_of((places[0, s] // 2) * width, width)
         made = dot(grad_low, weights[0, pl.ds(first, width), :], ((1,), (1,))).astype(BF16)
-        if width < grad_attended[s].shape[1]:
-            grad_attended[s][:, PAIR:] = jnp.zeros((ROWS, PAIR), BF16)
-        grad_attended[s][:, :width] = made
+        grad_attended[s][...] = made
 
 
 def third_part(places, blocks, table, grad_second, grad_up, unit, inverse, slots, lanes):
@@ -1357,7 +1368,7 @@
     lines_two, grad_up = second_part(places, late_blocks, grad_down, slope)
     grad_second = after(grad_second, grad_up)
     made, grads = third_part(
-        places, blocks, table, grad_second, grad_up, unit, inverse, slots, query.shape[-1]
+        places, blocks, table, grad_second, grad_up, unit, inverse, slots, D // slots
     )
     lines_three, grad_first, grad_proj = made
     lines_two = lines_two + lines_three
@@ -1478,7 +1489,7 @@
         )
         qkv_wgrad = jnp.concatenate(by_chip(pieces), axis=1)
         ends = jnp.pad(
-            lax.dynamic_slice_in_dim(ends, core * share, share, 1), ((0, 30), (0, D - share))
+            lax.dynamic_slice_in_dim(ends, core * share, share, 1), ((0, 14), (0, D - share))
         )
         qkv_dp = SumDp(jnp.concatenate([qkv_wgrad.astype(F32), ends]))
         pack = jnp.concatenate([pack, come], axis=0)
@@ -1502,7 +1513,7 @@
         qkv_wgrad = whole_scatter(qkv_parts[0][None, : 3 * D], 3)
         ends = sum_seq(qkv_parts[0][3 * D : 3 * D + 2].astype(F32))
         ends = lax.dynamic_slice_in_dim(ends, me * share, share, 1)
-        qkv_wgrad = sum_dp(jnp.concatenate([qkv_wgrad, jnp.pad(ends, ((0, 30), (0, D - share)))]))
+        qkv_wgrad = sum_dp(jnp.concatenate([qkv_wgrad, jnp.pad(ends, ((0, 14), (0, D - share)))]))
         down_wgrad = sum_dp(whole_scatter(down_parts[0], 1))
         up_wgrad = sum_dp(whole_scatter(up_parts[0], 5))
     proj_wgrad = up_wgrad[4 * share :]

time: 263 us -> 263 us (level)
  no operation moved by 1% of the time
where the time goes in v2:
time: 263 us; the launch traced here: 260 us
  Pallas kernels  106 us (40%)
  starting transfers between devices  62 us (24%)
  waiting for transfers between devices  55.5 us (21%)
  other arithmetic  16.4 us (6%)
  local copies, waits for them, and re-layouts  15.1 us (6%)
    ppermute x65, starting transfers between devices, swap(): return lax.ppermute(value, ('dp', 'seq'), pairs)  62 us
    ppermute x65, waiting for transfers between devices, swap(): return lax.ppermute(value, ('dp', 'seq'), pairs)  55.5 us
    pallas_call x2, Pallas kernels, attend_back(): call(functools.partial(attend_back_kernel, len(keyvals), docs, heads, Non...  24.9 us
    pallas_call x1, Pallas kernels, first_part(): call(functools.partial(first_kernel, count, slots, groups), 'forward_up',...  14.5 us
    pallas_call x1, Pallas kernels, attend(): call(functools.partial(attend_kernel, len(keyvals), docs, slots > 1), 'at...  11.5 us
    pallas_call x2, Pallas kernels, gradient_call(): call(body, name, micros, out_shape=outs, in_specs=[ANY] * len(ins), out_s...  10.6 us
    pallas_call x1, Pallas kernels, head_part(): call(functools.partial(head_kernel, count, docs), 'head', 7, out_shape=ou...  9.11 us
    unnamed x140, local copies, waits for them, and re-layouts  9.1 us
  transfers between devices with their start and end apart: 65, of which 18 were waited for; matrix products, arithmetic and copies ran while one was open for 9% of the time, Pallas kernels for 41%

profile of v2, /device:TPU:0, one launch (start us, length us, event | category | flops | bytes accessed | tf_op | source)
XLA Modules:
  0.0 259.7 jit_solution(7785578925376761446)
XLA Ops:
  0.7 3.0 %collective-permute-start.2 = (bf16[256,768]{1,0:T(8,128)(2,1)}, bf16[256,768]{1,0:T(8,128)(2,1)S(1)}, u32[]{:S(2)}, u32[]{:S(2)}) collective-permute-start(bf16[256,768]{1,0:T(8,128)(2,1)} %bitcast.28.refs_0_.refs_12_), channel_id=1, source_target_pairs={{0,2},{1,3},{2,0},{3,1},{4,6},{5,7},{6,4},{7,5},{8,10},{9,11},{10,... | collective-permute-start | bytes 1179656 | tf_op jit(solution)/shard_map/ppermute | solution.py:35
  6.7 2.0 collective-permute-start.6
  15.4 3.2 %collective-permute-done.7 = bf16[3,96,192]{2,1,0:T(8,128)(2,1)S(1)} collective-permute-done((bf16[3,96,192]{2,1,0:T(8,128)(2,1)S(1)}, bf16[3,96,192]{2,1,0:T(8,128)(2,1)S(1)}, u32[]{:S(2)}, u32[]{:S(2)}) %collective-permute-start.7) | collective-permute-done | bytes 110624 | tf_op jit(solution)/shard_map/ppermute | solution.py:35
  18.6 2.3 collective-permute-done.6
  26.3 8.1 %collective-permute-done.4.refs_3_ = bf16[256,768]{1,0:T(8,128)(2,1)} collective-permute-done((bf16[256,768]{1,0:T(8,128)(2,1)}, bf16[256,768]{1,0:T(8,128)(2,1)}, u32[]{:S(2)}, u32[]{:S(2)}) %collective-permute-start.4) | collective-permute-done | bytes 393248 | tf_op jit(solution)/shard_map/ppermute | solution.py:35
  35.2 5.4 %qkv.1 = (bf16[4,256,256]{2,1,0:T(8,128)(2,1)}, bf16[2,4,256,256]{3,2,1,0:T(8,128)(2,1)}) custom-call(s32[3,8]{1,0:T(4,128)} %pad_add_fusion.places, bf16[256,768]{1,0:T(8,128)(2,1)} %bitcast.28.refs_0_.refs_12_, bf16[256,768]{1,0:T(8,128)(2,1)} %copy-done.56, bf16[256,768]{1,0:T(8,128)(2,1)} %collective-permute-done.3.refs_2_, ...), custom_call_target="tpu_custom_call" | custom-call | flops 5500000256 | bytes 5000000 | tf_op jit(solution)/shard_map/qkv/pallas_call | solution.py:259
  40.6 3.2 %turn_tokens.1.refs_0_ = bf16[768,1024]{1,0:T(8,128)(2,1)} custom-call(bf16[256,768]{1,0:T(8,128)(2,1)} %bitcast.28.refs_0_.refs_12_, bf16[256,768]{1,0:T(8,128)(2,1)} %copy-done.56, bf16[256,768]{1,0:T(8,128)(2,1)} %collective-permute-done.3.refs_2_, bf16[256,768]{1,0:T(8,128)(2,1)} %collective-permute-done.4.refs_3_), custom_call_target="tpu_custom_call" | custom-call | flops 2200000000 | bytes 2000000 | tf_op jit(solution)/shard_map/turn_tokens/pallas_call | solution.py:279
  43.8 5.9 %collective-permute-done.1.refs_1_ = bf16[480,768]{1,0:T(8,128)(2,1)} collective-permute-done((bf16[480,768]{1,0:T(8,128)(2,1)S(1)}, bf16[480,768]{1,0:T(8,128)(2,1)}, u32[]{:S(2)}, u32[]{:S(2)}) %collective-permute-start.1) | collective-permute-done | bytes 737312 | tf_op jit(solution)/shard_map/ppermute | solution.py:35
  55.3 11.5 %attend.1 = (f32[4,256,256]{2,1,0:T(8,128)}, f32[4,256,256]{2,1,0:T(8,128)}, bf16[256,256]{1,0:T(8,128)(2,1)}, bf16[256,256]{1,0:T(8,128)(2,1)}, bf16[256,256]{1,0:T(8,128)(2,1)}, /*index=5*/bf16[256,256]{1,0:T(8,128)(2,1)}) custom-call(bf16[4,256,256]{2,1,0:T(8,128)(2,1)} %get-tuple-element.274.refs_0_, ...), custom_call_target="tpu_custom_call" | custom-call | flops 13200000000 | bytes 12000000 | tf_op jit(solution)/shard_map/attend/pallas_call | solution.py:417
  66.8 3.1 %collective-permute-done.12.refs_2_ = bf16[496,768]{1,0:T(8,128)(2,1)S(1)} collective-permute-done((bf16[496,768]{1,0:T(8,128)(2,1)S(1)}, bf16[496,768]{1,0:T(8,128)(2,1)S(1)}, u32[]{:S(2)}, u32[]{:S(2)}) %collective-permute-start.12) | collective-permute-done | bytes 761888 | tf_op jit(solution)/shard_map/ppermute | solution.py:35
  75.0 2.5 collective-permute-done.16.refs_9_
  77.6 3.7 %collective-permute-done.17.refs_10_ = bf16[256,256]{1,0:T(8,128)(2,1)S(1)} collective-permute-done((bf16[256,256]{1,0:T(8,128)(2,1)}, bf16[256,256]{1,0:T(8,128)(2,1)S(1)}, u32[]{:S(2)}, u32[]{:S(2)}) %collective-permute-start.17) | collective-permute-done | bytes 131104 | tf_op jit(solution)/shard_map/ppermute | solution.py:35
  84.1 14.5 %forward_up.1 = (f32[16,768]{1,0:T(8,128)}, f32[256,768]{1,0:T(8,128)}, f32[256,1]{1,0:T(8,128)}, bf16[256,3072]{1,0:T(8,128)(2,1)}, bf16[256,3072]{1,0:T(8,128)...) custom-call(s32[3,8]{1,0:T(4,128)} %pad_add_fusion.places, bf16[496,768]{1,0:T(8,128)(2,1)} %copy-done.7, ...), custom_call_target="tpu_custom_call" | custom-call | flops 12099999744 | bytes 11000000 | tf_op jit(solution)/shard_map/forward_up/pallas_call | solution.py:742
  99.3 2.0 collective-permute-done.25.refs_7_
  102.2 9.1 %head.1 = (bf16[256,768]{1,0:T(8,128)(2,1)}, f32[8,768]{1,0:T(8,128)}, f32[8,2432]{1,0:T(8,128)}, f32[256,768]{1,0:T(8,128)}, bf16[256,768]{1,0:T(8,128)(2,1)}) custom-call(s32[3,8]{1,0:T(4,128)} %pad_add_fusion.places, bf16[480,768]{1,0:T(8,128)(2,1)} %copy-done.12, bf16[480,768]{1,0:T(8,128)(2,1)} %collective-permute-done.1.refs_1_, ...), custom_call_target="tpu_custom_call" | custom-call | flops 7699999744 | bytes 7000000 | tf_op jit(solution)/shard_map/head/pallas_call | solution.py:837
  115.1 4.8 %down_gradient.1 = (bf16[2,192,768]{2,1,0:T(8,128)(2,1)}, bf16[2,192,768]{2,1,0:T(8,128)(2,1)}, bf16[192,768]{1,0:T(8,128)(2,1)}, bf16[192,768]{1,0:T(8,128)(2,1)}, f32[384,768]{1,0:T(8,128)}) custom-call(bf16[2304,256]{1,0:T(8,128)(2,1)} %get-tuple-element.218.refs_0_, bf16[2304,256]{1,0:T(8,128)(2,1)} %copy-done.40, ...), custom_call_target="tpu_custom_call" | custom-call | flops 3300000000 | bytes 3000000 | tf_op jit(solution)/shard_map/down_gradient/pallas_call | solution.py:967
  122.3 7.1 %backward_down.1 = (f32[8,768]{1,0:T(8,128)}, bf16[4,256,768]{2,1,0:T(8,128)(2,1)}) custom-call(s32[3,8]{1,0:T(4,128)} %pad_add_fusion.places, bf16[480,768]{1,0:T(8,128)(2,1)} %copy-done.12, bf16[480,768]{1,0:T(8,128)(2,1)} %collective-permute-done.1.refs_1_, bf16[480,768]{1,0:T(8,128)(2,1)} %collective-permute-done.10.refs_2_, ...), custom_call_target="tpu_custom_call" | custom-call | flops 5500000256 | bytes 5000000 | tf_op jit(solution)/shard_map/backward_down/pallas_call | solution.py:873
  129.6 7.9 %backward_up.1 = (f32[8,768]{1,0:T(8,128)}, f32[256,768]{1,0:T(8,128)}, bf16[256,768]{1,0:T(8,128)(2,1)}, bf16[256,192]{1,0:T(8,128)(2,1)}, bf16[256,192]{1,0:T(...) custom-call(s32[3,8]{1,0:T(4,128)} %pad_add_fusion.places, bf16[496,768]{1,0:T(8,128)(2,1)} %copy-done.7, ...), custom_call_target="tpu_custom_call" | custom-call | flops 7699999744 | bytes 7000000 | tf_op jit(solution)/shard_map/backward_up/pallas_call | solution.py:927
  145.1 5.8 %up_gradient.1 = (bf16[2,240,768]{2,1,0:T(8,128)(2,1)}, bf16[2,240,768]{2,1,0:T(8,128)(2,1)}, bf16[240,768]{1,0:T(8,128)(2,1)}, bf16[240,768]{1,0:T(8,128)(2,1)}, f32[480,768]{1,0:T(8,128)}) custom-call(bf16[2304,256]{1,0:T(8,128)(2,1)} %get-tuple-element.218.refs_0_, bf16[2304,256]{1,0:T(8,128)(2,1)} %copy-done.40, ...), custom_call_target="tpu_custom_call" | custom-call | flops 4400000000 | bytes 4000000 | tf_op jit(solution)/shard_map/up_gradient/pallas_call | solution.py:967
  150.9 3.4 %collective-permute-done.36 = bf16[192,768]{1,0:T(8,128)(2,1)S(1)} collective-permute-done((bf16[192,768]{1,0:T(8,128)(2,1)S(1)}, bf16[192,768]{1,0:T(8,128)(2,1)S(1)}, u32[]{:S(2)}, u32[]{:S(2)}) %collective-permute-start.36) | collective-permute-done | bytes 294944 | tf_op jit(solution)/shard_map/ppermute | solution.py:35
  154.6 2.2 collective-permute-start.39
  158.5 15.4 %attend_back.2 = (bf16[4,256,128]{2,1,0:T(8,128)(2,1)}, bf16[2,4,256,128]{3,2,1,0:T(8,128)(2,1)}, bf16[2,4,256,128]{3,2,1,0:T(8,128)(2,1)}) custom-call(bf16[4,256,256]{2,1,0:T(8,128)(2,1)} %get-tuple-element.274.refs_0_, f32[4,256,256]{2,1,0:T(8,128)} %get-tuple-element.216.refs_1_, f32[4,256,256]{2,1,0:T(8,128)} %get-tuple-element.217.refs_2_, ...), custom_call_target="tpu_custom_call" | custom-call | flops 16499999744 | bytes 15000000 | tf_op jit(solution)/shard_map/attend_back/pallas_call | solution.py:514
  179.5 2.7 %collective-permute-start.45 = (bf16[192,768]{1,0:T(8,128)(2,1)S(1)}, bf16[192,768]{1,0:T(8,128)(2,1)S(1)}, u32[]{:S(2)}, u32[]{:S(2)}) collective-permute-start(bf16[192,768]{1,0:T(8,128)(2,1)S(1)} %add_convert_fusion.3), channel_id=1, source_target_pairs={{0,24},{1,25},{2,26},{3,27},{4,28},{5,29},{6,30},{7,31},{8,16},{9,... | collective-permute-start | bytes 884744 | tf_op jit(solution)/shard_map/ppermute | solution.py:35
  182.2 9.6 %attend_back.3 = (bf16[4,256,128]{2,1,0:T(8,128)(2,1)}, bf16[2,4,256,128]{3,2,1,0:T(8,128)(2,1)}, bf16[2,4,256,128]{3,2,1,0:T(8,128)(2,1)}) custom-call(bf16[4,256,256]{2,1,0:T(8,128)(2,1)} %get-tuple-element.274.refs_0_, f32[4,256,256]{2,1,0:T(8,128)} %get-tuple-element.216.refs_1_, f32[4,256,256]{2,1,0:T(8,128)} %get-tuple-element.217.refs_2_, ...), custom_call_target="tpu_custom_call" | custom-call | flops 8800000000 | bytes 8000000 | tf_op jit(solution)/shard_map/attend_back/pallas_call | solution.py:514
  193.6 2.3 collective-permute-start.49
  195.9 6.3 %input_weights.1 = (bf16[1168,256]{1,0:T(8,128)(2,1)}, bf16[1168,256]{1,0:T(8,128)(2,1)}) custom-call(s32[3,8]{1,0:T(4,128)} %pad_add_fusion.places, bf16[768,1024]{1,0:T(8,128)(2,1)} %turn_tokens.1.refs_0_, bf16[768,1024]{1,0:T(8,128)(2,1)} %collective-permute-done.26.refs_1_, bf16[4,256,128]{2,1,0:T(8,128)(2,1)} %get-tuple-element.257.refs_2_, ...), custom_call_target="tpu_custom_call" | custom-call | flops 5500000256 | bytes 5000000 | tf_op jit(solution)/shard_map/input_weights/pallas_call | solution.py:1115
  202.3 2.7 %collective-permute-done.49 = bf16[240,768]{1,0:T(8,128)(2,1)} collective-permute-done((bf16[240,768]{1,0:T(8,128)(2,1)S(1)}, bf16[240,768]{1,0:T(8,128)(2,1)}, u32[]{:S(2)}, u32[]{:S(2)}) %collective-permute-start.49) | collective-permute-done | bytes 368672 | tf_op jit(solution)/shard_map/ppermute | solution.py:35
  207.5 2.7 %collective-permute-start.56 = (bf16[240,768]{1,0:T(8,128)(2,1)S(1)}, bf16[240,768]{1,0:T(8,128)(2,1)S(1)}, u32[]{:S(2)}, u32[]{:S(2)}) collective-permute-start(bf16[240,768]{1,0:T(8,128)(2,1)S(1)} %add_convert_fusion.1), channel_id=1, source_target_pairs={{0,24},{1,25},{2,26},{3,27},{4,28},{5,29},{6,30},{7,31},{8,16},{9,... | collective-permute-start | bytes 1105928 | tf_op jit(solution)/shard_map/ppermute | solution.py:35
  217.3 5.8 %input_gradients.1 = (f32[256,768]{1,0:T(8,128)}, bf16[256,768]{1,0:T(8,128)(2,1)}, bf16[256,768]{1,0:T(8,128)(2,1)}, bf16[256,768]{1,0:T(8,128)(2,1)}) custom-call(s32[3,8]{1,0:T(4,128)} %pad_add_fusion.places, bf16[4,3,96,256]{3,2,1,0:T(8,128)(2,1)} %copy-done.10, bf16[4,3,96,256]{3,2,1,0:T(8,128)(2,1)} %copy-done.53, ...), custom_call_target="tpu_custom_call" | custom-call | flops 5500000256 | bytes 5000000 | tf_op jit(solution)/shard_map/input_gradients/pallas_call | solution.py:1172
  227.4 6.1 %collective-permute-done.61 = f32[16,1376]{1,0:T(8,128)S(1)} collective-permute-done((f32[16,1376]{1,0:T(8,128)S(1)}, f32[16,1376]{1,0:T(8,128)S(1)}, u32[]{:S(2)}, u32[]{:S(2)}) %collective-permute-start.61) | collective-permute-done | bytes 88096 | tf_op jit(solution)/shard_map/ppermute | solution.py:35
  241.8 2.8 %collective-permute-start.64 = (bf16[240,768]{1,0:T(8,128)(2,1)S(1)}, bf16[240,768]{1,0:T(8,128)(2,1)S(1)}, u32[]{:S(2)}, u32[]{:S(2)}) collective-permute-start(bf16[240,768]{1,0:T(8,128)(2,1)S(1)} %add_convert_fusion), channel_id=1, source_target_pairs={{0,8},{1,9},{2,10},{3,11},{4,12},{5,13},{6,14},{7,15},{8,0},{9,1},... | collective-permute-start | bytes 1105928 | tf_op jit(solution)/shard_map/ppermute | solution.py:35
  248.9 5.7 %collective-permute-done.64 = bf16[240,768]{1,0:T(8,128)(2,1)S(1)} collective-permute-done((bf16[240,768]{1,0:T(8,128)(2,1)S(1)}, bf16[240,768]{1,0:T(8,128)(2,1)S(1)}, u32[]{:S(2)}, u32[]{:S(2)}) %collective-permute-start.64) | collective-permute-done | bytes 368672 | tf_op jit(solution)/shard_map/ppermute | solution.py:35
  (351 shorter events, 84.7 us)
Async XLA Ops:
  0.7 20.3 %collective-permute-start.2 = (bf16[256,768]{1,0:T(8,128)(2,1)}, bf16[256,768]{1,0:T(8,128)(2,1)S(1)}, u32[]{:S(2)}, u32[]{:S(2)}) collective-permute-start(bf16[256,768]{1,0:T(8,128)(2,1)} %bitcast.28.refs_0_.refs_12_), channel_id=1, source_target_pairs={{0,2},{1,3},{2,0},{3,1},{4,6},{5,7},{6,4},{7,5},{8,10},{9,11},{10,... | collective-permute-start | bytes 1179656 | tf_op jit(solution)/shard_map/ppermute | solution.py:35
  3.7 17.3 %collective-permute-start.3 = (bf16[256,768]{1,0:T(8,128)(2,1)}, bf16[256,768]{1,0:T(8,128)(2,1)}, u32[]{:S(2)}, u32[]{:S(2)}) collective-permute-start(bf16[256,768]{1,0:T(8,128)(2,1)} %bitcast.28.refs_0_.refs_12_), channel_id=1, source_target_pairs={{0,4},{1,5},{2,6},{3,7},{4,0},{5,1},{6,2},{7,3},{8,12},{9,13},{10,... | collective-permute-start | bytes 1179656 | tf_op jit(solution)/shard_map/ppermute | solution.py:35
  6.7 14.1 %collective-permute-start.6 = (bf16[3,96,192]{2,1,0:T(8,128)(2,1)S(1)}, bf16[3,96,192]{2,1,0:T(8,128)(2,1)S(1)}, u32[]{:S(2)}, u32[]{:S(2)}) collective-permute-start(bf16[3,96,192]{2,1,0:T(8,128)(2,1)S(1)} %get-tuple-element.401), channel_id=1, source_target_pairs={{0,4},{1,5},{2,6},{3,7},{4,0},{5,1},{6,2},{7,3},{8,12},{9,13},{10,... | collective-permute-start | bytes 331784 | tf_op jit(solution)/shard_map/ppermute | solution.py:35
  24.1 26.1 %collective-permute-start = (bf16[496,768]{1,0:T(8,128)(2,1)S(1)}, bf16[496,768]{1,0:T(8,128)(2,1)S(1)}, u32[]{:S(2)}, u32[]{:S(2)}) collective-permute-start(bf16[496,768]{1,0:T(8,128)(2,1)S(1)} %pad_maximum_fusion.refs_0_), channel_id=1, source_target_pairs={{0,2},{1,3},{2,0},{3,1},{4,6},{5,7},{6,4},{7,5},{8,12},{9,13},{10,... | collective-permute-start | bytes 2285576 | tf_op jit(solution)/shard_map/ppermute | solution.py:35
  25.7 23.9 %collective-permute-start.1 = (bf16[480,768]{1,0:T(8,128)(2,1)S(1)}, bf16[480,768]{1,0:T(8,128)(2,1)}, u32[]{:S(2)}, u32[]{:S(2)}) collective-permute-start(bf16[480,768]{1,0:T(8,128)(2,1)S(1)} %constant_dynamic-update-slice_fusion.refs_0_), channel_id=1, source_target_pairs={{0,4},{1,5},{2,6},{3,7},{4,0},{5,1},{6,2},{7,3},{8,10},{9,11},{10,... | collective-permute-start | bytes 2211848 | tf_op jit(solution)/shard_map/ppermute | solution.py:35
  50.2 16.6 %collective-permute-start.14 = (bf16[496,768]{1,0:T(8,128)(2,1)S(1)}, bf16[496,768]{1,0:T(8,128)(2,1)S(1)}, u32[]{:S(2)}, u32[]{:S(2)}) collective-permute-start(bf16[496,768]{1,0:T(8,128)(2,1)S(1)} %pad_maximum_fusion.refs_0_), channel_id=1, source_target_pairs={{0,1},{1,0},{2,3},{3,2},{4,5},{5,4},{6,7},{7,6},{8,9},{9,8},{10,11... | collective-permute-start | bytes 2285576 | tf_op jit(solution)/shard_map/ppermute | solution.py:35
  50.7 23.1 %collective-permute-start.10 = (bf16[480,768]{1,0:T(8,128)(2,1)}, bf16[480,768]{1,0:T(8,128)(2,1)}, u32[]{:S(2)}, u32[]{:S(2)}) collective-permute-start(bf16[480,768]{1,0:T(8,128)(2,1)} %collective-permute-done.1.refs_1_), channel_id=1, source_target_pairs={{0,2},{1,3},{2,0},{3,1},{4,6},{5,7},{6,4},{7,5},{8,12},{9,13},{10,... | collective-permute-start | bytes 2211848 | tf_op jit(solution)/shard_map/ppermute | solution.py:35
  51.2 18.7 %collective-permute-start.12 = (bf16[496,768]{1,0:T(8,128)(2,1)S(1)}, bf16[496,768]{1,0:T(8,128)(2,1)S(1)}, u32[]{:S(2)}, u32[]{:S(2)}) collective-permute-start(bf16[496,768]{1,0:T(8,128)(2,1)S(1)} %collective-permute-done.refs_1_), channel_id=1, source_target_pairs={{0,4},{1,5},{2,6},{3,7},{4,0},{5,1},{6,2},{7,3},{8,10},{9,11},{10,... | collective-permute-start | bytes 2285576 | tf_op jit(solution)/shard_map/ppermute | solution.py:35
  52.3 18.6 %collective-permute-start.13 = (bf16[496,768]{1,0:T(8,128)(2,1)S(1)}, bf16[496,768]{1,0:T(8,128)(2,1)S(1)}, u32[]{:S(2)}, u32[]{:S(2)}) collective-permute-start(bf16[496,768]{1,0:T(8,128)(2,1)S(1)} %collective-permute-done.refs_1_), channel_id=1, source_target_pairs={{0,8},{1,9},{2,10},{3,11},{4,12},{5,13},{6,14},{7,15},{8,0},{9,1},... | collective-permute-start | bytes 2285576 | tf_op jit(solution)/shard_map/ppermute | solution.py:35
  54.2 16.7 %collective-permute-start.15 = (bf16[496,768]{1,0:T(8,128)(2,1)S(1)}, bf16[496,768]{1,0:T(8,128)(2,1)S(1)}, u32[]{:S(2)}, u32[]{:S(2)}) collective-permute-start(bf16[496,768]{1,0:T(8,128)(2,1)S(1)} %collective-permute-done.refs_1_), channel_id=1, source_target_pairs={{0,1},{1,0},{2,3},{3,2},{4,5},{5,4},{6,7},{7,6},{8,9},{9,8},{10,11... | collective-permute-start | bytes 2285576 | tf_op jit(solution)/shard_map/ppermute | solution.py:35
  81.2 17.3 %collective-permute-start.19 = (bf16[480,768]{1,0:T(8,128)(2,1)S(1)}, bf16[480,768]{1,0:T(8,128)(2,1)}, u32[]{:S(2)}, u32[]{:S(2)}) collective-permute-start(bf16[480,768]{1,0:T(8,128)(2,1)S(1)} %constant_dynamic-update-slice_fusion.refs_0_), channel_id=1, source_target_pairs={{0,2},{1,3},{2,0},{3,1},{4,6},{5,7},{6,4},{7,5},{8,12},{9,13},{10,... | collective-permute-start | bytes 2211848 | tf_op jit(solution)/shard_map/ppermute | solution.py:35
  81.8 16.8 %collective-permute-start.20 = (bf16[480,768]{1,0:T(8,128)(2,1)S(1)}, bf16[480,768]{1,0:T(8,128)(2,1)}, u32[]{:S(2)}, u32[]{:S(2)}) collective-permute-start(bf16[480,768]{1,0:T(8,128)(2,1)S(1)} %constant_dynamic-update-slice_fusion.refs_0_), channel_id=1, source_target_pairs={{0,1},{1,0},{2,3},{3,2},{4,5},{5,4},{6,7},{7,6},{8,9},{9,8},{10,11... | collective-permute-start | bytes 2211848 | tf_op jit(solution)/shard_map/ppermute | solution.py:35
  81.8 16.8 %collective-permute-start.21 = (bf16[480,768]{1,0:T(8,128)(2,1)}, bf16[480,768]{1,0:T(8,128)(2,1)}, u32[]{:S(2)}, u32[]{:S(2)}) collective-permute-start(bf16[480,768]{1,0:T(8,128)(2,1)} %collective-permute-done.1.refs_1_), channel_id=1, source_target_pairs={{0,1},{1,0},{2,3},{3,2},{4,5},{5,4},{6,7},{7,6},{8,9},{9,8},{10,11... | collective-permute-start | bytes 2211848 | tf_op jit(solution)/shard_map/ppermute | solution.py:35
  82.3 16.3 %collective-permute-start.22 = (bf16[480,768]{1,0:T(8,128)(2,1)}, bf16[480,768]{1,0:T(8,128)(2,1)}, u32[]{:S(2)}, u32[]{:S(2)}) collective-permute-start(bf16[480,768]{1,0:T(8,128)(2,1)} %collective-permute-done.10.refs_2_), channel_id=1, source_target_pairs={{0,1},{1,0},{2,3},{3,2},{4,5},{5,4},{6,7},{7,6},{8,9},{9,8},{10,11... | collective-permute-start | bytes 2211848 | tf_op jit(solution)/shard_map/ppermute | solution.py:35
  98.7 23.6 %collective-permute-start.26 = (bf16[768,1024]{1,0:T(8,128)(2,1)S(1)}, bf16[768,1024]{1,0:T(8,128)(2,1)}, u32[]{:S(2)}, u32[]{:S(2)}) collective-permute-start(bf16[768,1024]{1,0:T(8,128)(2,1)S(1)} %copy-done.38), channel_id=1, source_target_pairs={{0,1},{1,0},{2,3},{3,2},{4,5},{5,4},{6,7},{7,6},{8,9},{9,8},{10,11... | collective-permute-start | bytes 4718600 | tf_op jit(solution)/shard_map/ppermute | solution.py:35
  99.2 14.1 %collective-permute-start.27 = (bf16[2304,256]{1,0:T(8,128)(2,1)}, bf16[2304,256]{1,0:T(8,128)(2,1)S(1)}, u32[]{:S(2)}, u32[]{:S(2)}) collective-permute-start(bf16[2304,256]{1,0:T(8,128)(2,1)} %get-tuple-element.219), channel_id=1, source_target_pairs={{0,1},{1,0},{2,3},{3,2},{4,5},{5,4},{6,7},{7,6},{8,9},{9,8},{10,11... | collective-permute-start | bytes 3538952 | tf_op jit(solution)/shard_map/ppermute | solution.py:35
  119.9 18.4 %collective-permute-start.30 = (bf16[2,192,768]{2,1,0:T(8,128)(2,1)}, bf16[2,192,768]{2,1,0:T(8,128)(2,1)S(1)}, u32[]{:S(2)}, u32[]{:S(2)}) collective-permute-start(bf16[2,192,768]{2,1,0:T(8,128)(2,1)} %get-tuple-element.221), channel_id=1, source_target_pairs={{0,2},{1,3},{2,0},{3,1},{4,6},{5,7},{6,4},{7,5},{8,10},{9,11},{10,... | collective-permute-start | bytes 1769480 | tf_op jit(solution)/shard_map/ppermute | solution.py:35
  121.5 16.8 %collective-permute-start.31 = (bf16[2,192,768]{2,1,0:T(8,128)(2,1)}, bf16[2,192,768]{2,1,0:T(8,128)(2,1)S(1)}, u32[]{:S(2)}, u32[]{:S(2)}) collective-permute-start(bf16[2,192,768]{2,1,0:T(8,128)(2,1)} %get-tuple-element.222), channel_id=1, source_target_pairs={{0,4},{1,5},{2,6},{3,7},{4,0},{5,1},{6,2},{7,3},{8,12},{9,13},{10,... | collective-permute-start | bytes 1769480 | tf_op jit(solution)/shard_map/ppermute | solution.py:35
  129.5 14.4 %collective-permute-start.29 = (bf16[4,256,768]{2,1,0:T(8,128)(2,1)}, bf16[4,256,768]{2,1,0:T(8,128)(2,1)S(1)}, u32[]{:S(2)}, u32[]{:S(2)}) collective-permute-start(bf16[4,256,768]{2,1,0:T(8,128)(2,1)} %get-tuple-element.228.refs_10_.refs_2_), channel_id=1, source_target_pairs={{0,1},{1,0},{2,3},{3,2},{4,5},{5,4},{6,7},{7,6},{8,9},{9,8},{10,11... | collective-permute-start | bytes 4718600 | tf_op jit(solution)/shard_map/ppermute | solution.py:35
  154.3 19.5 %collective-permute-start.38 = (f32[8,3968]{1,0:T(8,128)S(1)}, f32[8,3968]{1,0:T(8,128)S(1)}, u32[]{:S(2)}, u32[]{:S(2)}) collective-permute-start(f32[8,3968]{1,0:T(8,128)S(1)} %pad_maximum_fusion.5), channel_id=1, source_target_pairs={{0,1},{1,0},{2,3},{3,2},{4,5},{5,4},{6,7},{7,6},{8,9},{9,8},{10,11... | collective-permute-start | bytes 380936 | tf_op jit(solution)/shard_map/ppermute | solution.py:35
  154.6 19.2 %collective-permute-start.39 = (bf16[192,768]{1,0:T(8,128)(2,1)S(1)}, bf16[192,768]{1,0:T(8,128)(2,1)S(1)}, u32[]{:S(2)}, u32[]{:S(2)}) collective-permute-start(bf16[192,768]{1,0:T(8,128)(2,1)S(1)} %select_convert_fusion.2), channel_id=1, source_target_pairs={{0,8},{1,9},{2,10},{3,11},{4,12},{5,13},{6,14},{7,15},{8,0},{9,1},... | collective-permute-start | bytes 884744 | tf_op jit(solution)/shard_map/ppermute | solution.py:35
  156.8 18.6 %collective-permute-start.40 = (bf16[2,240,768]{2,1,0:T(8,128)(2,1)S(1)}, bf16[2,240,768]{2,1,0:T(8,128)(2,1)S(1)}, u32[]{:S(2)}, u32[]{:S(2)}) collective-permute-start(bf16[2,240,768]{2,1,0:T(8,128)(2,1)S(1)} %copy-done.52), channel_id=1, source_target_pairs={{0,2},{1,3},{2,0},{3,1},{4,6},{5,7},{6,4},{7,5},{8,10},{9,11},{10,... | collective-permute-start | bytes 2211848 | tf_op jit(solution)/shard_map/ppermute | solution.py:35
  157.3 18.3 %collective-permute-start.41 = (bf16[2,240,768]{2,1,0:T(8,128)(2,1)S(1)}, bf16[2,240,768]{2,1,0:T(8,128)(2,1)S(1)}, u32[]{:S(2)}, u32[]{:S(2)}) collective-permute-start(bf16[2,240,768]{2,1,0:T(8,128)(2,1)S(1)} %copy-done.51), channel_id=1, source_target_pairs={{0,4},{1,5},{2,6},{3,7},{4,0},{5,1},{6,2},{7,3},{8,12},{9,13},{10,... | collective-permute-start | bytes 2211848 | tf_op jit(solution)/shard_map/ppermute | solution.py:35
  175.6 16.2 %collective-permute-start.42 = (f32[8,3968]{1,0:T(8,128)S(1)}, f32[8,3968]{1,0:T(8,128)S(1)}, u32[]{:S(2)}, u32[]{:S(2)}) collective-permute-start(f32[8,3968]{1,0:T(8,128)S(1)} %add.230), channel_id=1, source_target_pairs={{0,2},{1,3},{2,0},{3,1},{4,6},{5,7},{6,4},{7,5},{8,10},{9,11},{10,... | collective-permute-start | bytes 380936 | tf_op jit(solution)/shard_map/ppermute | solution.py:35
  177.3 14.5 %collective-permute-start.43 = (bf16[240,768]{1,0:T(8,128)(2,1)S(1)}, bf16[240,768]{1,0:T(8,128)(2,1)S(1)}, u32[]{:S(2)}, u32[]{:S(2)}) collective-permute-start(bf16[240,768]{1,0:T(8,128)(2,1)S(1)} %fusion.7), channel_id=1, source_target_pairs={{0,4},{1,5},{2,6},{3,7},{4,0},{5,1},{6,2},{7,3},{8,12},{9,13},{10,... | collective-permute-start | bytes 1105928 | tf_op jit(solution)/shard_map/ppermute | solution.py:35
  178.0 13.9 %collective-permute-start.44 = (bf16[240,768]{1,0:T(8,128)(2,1)S(1)}, bf16[240,768]{1,0:T(8,128)(2,1)S(1)}, u32[]{:S(2)}, u32[]{:S(2)}) collective-permute-start(bf16[240,768]{1,0:T(8,128)(2,1)S(1)} %fusion.6), channel_id=1, source_target_pairs={{0,2},{1,3},{2,0},{3,1},{4,6},{5,7},{6,4},{7,5},{8,10},{9,11},{10,... | collective-permute-start | bytes 1105928 | tf_op jit(solution)/shard_map/ppermute | solution.py:35
  182.2 20.0 %collective-permute-start.46 = (bf16[2,4,256,128]{3,2,1,0:T(8,128)(2,1)}, bf16[2,4,256,128]{3,2,1,0:T(8,128)(2,1)S(1)}, u32[]{:S(2)}, u32[]{:S(2)}) collective-permute-start(bf16[2,4,256,128]{3,2,1,0:T(8,128)(2,1)} %get-tuple-element.277.refs_5_), channel_id=1, source_target_pairs={{0,1},{1,0},{2,3},{3,2},{4,5},{5,4},{6,7},{7,6},{8,9},{9,8},{10,11... | collective-permute-start | bytes 1572872 | tf_op jit(solution)/shard_map/ppermute | solution.py:35
  207.5 29.4 %collective-permute-start.56 = (bf16[240,768]{1,0:T(8,128)(2,1)S(1)}, bf16[240,768]{1,0:T(8,128)(2,1)S(1)}, u32[]{:S(2)}, u32[]{:S(2)}) collective-permute-start(bf16[240,768]{1,0:T(8,128)(2,1)S(1)} %add_convert_fusion.1), channel_id=1, source_target_pairs={{0,24},{1,25},{2,26},{3,27},{4,28},{5,29},{6,30},{7,31},{8,16},{9,... | collective-permute-start | bytes 1105928 | tf_op jit(solution)/shard_map/ppermute | solution.py:35
  226.5 15.4 %collective-permute-start.62 = (bf16[192,768]{1,0:T(8,128)(2,1)S(1)}, bf16[192,768]{1,0:T(8,128)(2,1)S(1)}, u32[]{:S(2)}, u32[]{:S(2)}) collective-permute-start(bf16[192,768]{1,0:T(8,128)(2,1)S(1)} %add_convert_fusion.2), channel_id=1, source_target_pairs={{0,8},{1,9},{2,10},{3,11},{4,12},{5,13},{6,14},{7,15},{8,0},{9,1},... | collective-permute-start | bytes 884744 | tf_op jit(solution)/shard_map/ppermute | solution.py:35
  238.2 18.4 %collective-permute-start.59 = (bf16[256,768]{1,0:T(8,128)(2,1)}, bf16[256,768]{1,0:T(8,128)(2,1)S(1)}, u32[]{:S(2)}, u32[]{:S(2)}) collective-permute-start(bf16[256,768]{1,0:T(8,128)(2,1)} %get-tuple-element.324), channel_id=1, source_target_pairs={{0,6},{1,7},{2,4},{3,5},{4,2},{5,3},{6,0},{7,1},{8,14},{9,15},{10,... | collective-permute-start | bytes 1179656 | tf_op jit(solution)/shard_map/ppermute | solution.py:35
  239.6 17.0 %collective-permute-start.58 = (bf16[256,768]{1,0:T(8,128)(2,1)}, bf16[256,768]{1,0:T(8,128)(2,1)S(1)}, u32[]{:S(2)}, u32[]{:S(2)}) collective-permute-start(bf16[256,768]{1,0:T(8,128)(2,1)} %get-tuple-element.323), channel_id=1, source_target_pairs={{0,4},{1,5},{2,6},{3,7},{4,0},{5,1},{6,2},{7,3},{8,12},{9,13},{10,... | collective-permute-start | bytes 1179656 | tf_op jit(solution)/shard_map/ppermute | solution.py:35
  241.1 15.5 %collective-permute-start.57 = (bf16[256,768]{1,0:T(8,128)(2,1)}, bf16[256,768]{1,0:T(8,128)(2,1)S(1)}, u32[]{:S(2)}, u32[]{:S(2)}) collective-permute-start(bf16[256,768]{1,0:T(8,128)(2,1)} %get-tuple-element.322), channel_id=1, source_target_pairs={{0,2},{1,3},{2,0},{3,1},{4,6},{5,7},{6,4},{7,5},{8,10},{9,11},{10,... | collective-permute-start | bytes 1179656 | tf_op jit(solution)/shard_map/ppermute | solution.py:35
  (101 other events, 743.7 us)
